TPU v7x, 32 devices: a whole 2x2x4 slice. The times are simulated.
32 devices in a mesh: groups: 2 (over x), docs: 16 (over z, y, core).
Axes of the slice: x: 2, y: 2, z: 4, core: 2. Of those that a mesh axis runs over, the one named last changes fastest.
Arguments:
- embeddings: bfloat16 [4096, 1024], P(('groups', 'docs')), parts along dimension 0, may hold values from -100 to 100
- labels: int32 [4096], P(('groups', 'docs')), parts along dimension 0, may hold values from 0 to 15, as said below
- row_slot: int32 [4096], P(('groups', 'docs')), parts along dimension 0, may hold values from 0 to 2047, as said below
Outputs:
- density: float32 [4096], P(('groups', 'docs')), parts along dimension 0
- neighbour_mean: bfloat16 [4096, 1024], P(('groups', 'docs')), parts along dimension 0
There are 2 independent parts, one for each index of `groups`. A program takes and returns all parts, laid end to end along the dimension named above; each array names one. Nothing has to cross between parts.
Inputs may be any that keep to these rules, and one draw needn't show every extreme that they name: row_slot is a permutation of 0 to 2047; at most 16 documents of one device take rows of one block, and some device places exactly 16 documents in some block. All documents in one block share one label; documents with equal labels lie in blocks at most 3 apart, and some label spans 4 blocks.
All inputs are finite; a program needn't handle non-finite values.
Results may differ from a plain program's by a relative error of at most 0.0029.
Values may be sent and summed in bfloat16 or wider, within the bound.
A program may use at most 64 MiB of HBM per device.

v0:
```python
import functools
import math

import jax
import jax.numpy as jnp
from jax import lax
from jax.experimental import pallas as pl
from jax.experimental.pallas import tpu as pltpu
from jax.sharding import PartitionSpec as P

MESH = pl.DeviceIdType.MESH
CORES = 2
PIECES = 2
HALVES = 1

neg_large = -1e30
kernel_gain = 4.0


def chip_grid(device_count):
    chips = device_count // CORES
    fast = 1
    while (2 * fast) * (2 * fast) <= chips and chips % (2 * fast) == 0:
        fast *= 2
    return chips // fast, fast


def kernel(
    grid_slow, grid_fast, x_ref, lab_ref, dens_ref, mean_ref,
    buf, labs, mine, acc, row_max, row_total,
    send_sem, recv_sem, lsend_sem, lrecv_sem, own_sem, own_lab_sem,
):
    rows, width = x_ref.shape
    part = rows // PIECES
    group = PIECES // HALVES
    half_rows = rows // HALVES
    keys = CORES * half_rows
    me = lax.axis_index("docs")
    core = lax.rem(me, CORES)
    chip = me // CORES
    y = lax.rem(chip, grid_fast)
    z = chip // grid_fast

    def device(zz, yy, cc):
        return (zz * grid_fast + yy) * CORES + cc

    targets = (
        (z > 0, device(z - 1, y, core)),
        (z < grid_slow - 1, device(z + 1, y, core)),
        (y > 0, device(z, y - 1, core)),
        (y < grid_fast - 1, device(z, y + 1, core)),
        (z >= 0, device(z, y, 1 - core)),
    )

    barrier = pltpu.get_barrier_semaphore()
    for there, target in targets:
        @pl.when(there)
        def _():
            pl.semaphore_signal(barrier, inc=1, device_id={"docs": target}, device_id_type=MESH)

    def data_of(zz, yy, cc, piece):
        where = ((zz * grid_fast + yy) * HALVES + piece // group) * CORES + cc
        return buf.at[pl.ds(pl.multiple_of((where * group + lax.rem(piece, group)) * part, part), part)]

    own_copies = [pltpu.make_async_copy(x_ref, mine, own_sem.at[PIECES])]
    for piece in range(PIECES):
        own_copies.append(
            pltpu.make_async_copy(
                x_ref.at[pl.ds(piece * part, part)], data_of(z, y, core, piece), own_sem.at[piece]
            )
        )
    own_copies.append(pltpu.make_async_copy(lab_ref, labs.at[me], own_lab_sem.at[0]))
    for copy in own_copies:
        copy.start()
    pl.semaphore_wait(barrier, sum(there.astype(jnp.int32) for there, _ in targets))

    def data_copy(direction, zz, yy, piece, own):
        data = data_of(zz, yy, core, piece)
        return pltpu.make_async_remote_copy(
            x_ref.at[pl.ds(piece * part, part)] if own else data, data,
            send_sem.at[direction, (zz * grid_fast + yy) * PIECES + piece],
            recv_sem.at[device(zz, yy, core) * PIECES + piece],
            device_id={"docs": targets[direction][1]}, device_id_type=MESH,
        )

    def lab_copy(direction, zz, yy, own):
        slot = device(zz, yy, core)
        return pltpu.make_async_remote_copy(
            lab_ref if own else labs.at[slot], labs.at[slot],
            lsend_sem.at[direction, zz * grid_fast + yy], lrecv_sem.at[slot],
            device_id={"docs": targets[direction][1]}, device_id_type=MESH,
        )

    def each(directions, wanted, zz, yy, piece, own, act):
        for direction, want in zip(directions, wanted):
            @pl.when(jnp.logical_and(targets[direction][0], want))
            def _():
                @pl.when(piece == 0)
                def _():
                    act(lab_copy(direction, zz, yy, own))
                act(data_copy(direction, zz, yy, piece, own))

    start = lambda copy: copy.start()
    finish = lambda copy: copy.wait_send()

    def arrived(zz, yy, cc, piece):
        slot = device(zz, yy, cc)
        @pl.when(piece == 0)
        def _():
            pltpu.make_async_remote_copy(
                labs.at[slot], labs.at[slot], lsend_sem.at[0, 0], lrecv_sem.at[slot],
                device_id={"docs": targets[4][1]}, device_id_type=MESH,
            ).wait_recv()
        data = data_of(zz, yy, cc, piece)
        pltpu.make_async_remote_copy(
            data, data, send_sem.at[0, 0], recv_sem.at[slot * PIECES + piece],
            device_id={"docs": targets[4][1]}, device_id_type=MESH,
        ).wait_recv()

    yes = z >= 0
    for piece in range(PIECES):
        each((2, 3, 0, 1, 4), (yes,) * 5, z, y, piece, True, start)

    row_max[...] = jnp.full_like(row_max, neg_large)
    row_total[...] = jnp.zeros_like(row_total)
    acc[...] = jnp.zeros_like(acc)
    own_copies[-1].wait()
    label_column = jnp.transpose(
        jnp.broadcast_to(labs[me].astype(jnp.float32), (rows, rows))
    )[:, :1]
    column = lax.broadcasted_iota(jnp.int32, (rows, keys), 1)
    gap = (
        column + (column // half_rows) * (rows - half_rows)
        - lax.broadcasted_iota(jnp.int32, (rows, keys), 0)
    )
    for copy in own_copies[:-1]:
        copy.wait()

    def compute(zz, yy, half):
        where = zz * grid_fast + yy
        values = buf[pl.ds(pl.multiple_of((where * HALVES + half) * keys, keys), keys), :]
        tags = []
        for cc in range(CORES):
            tag = labs[where * CORES + cc].astype(jnp.float32)
            pieces = [tag[:, h * half_rows:(h + 1) * half_rows] for h in range(HALVES)]
            picked = pieces[0]
            for h in range(1, HALVES):
                picked = jnp.where(half == h, pieces[h], picked)
            tags.append(picked)
        tags = jnp.concatenate(tags, axis=1)
        scores = lax.dot_general(
            mine[...], values, (((1,), (1,)), ((), ())), preferred_element_type=jnp.float32
        ) * (kernel_gain / math.sqrt(width))
        self_gap = jnp.where(where == chip, core * rows - half * half_rows, CORES * rows)
        absorb(scores, (label_column == tags) & (gap != self_gap), values)

    def compute_core(zz, yy, cc):
        slot = device(zz, yy, cc)
        values = buf[pl.ds(pl.multiple_of(slot * rows, rows), rows), :]
        scores = lax.dot_general(
            mine[...], values, (((1,), (1,)), ((), ())), preferred_element_type=jnp.float32
        ) * (kernel_gain / math.sqrt(width))
        absorb(scores, label_column == labs[slot].astype(jnp.float32), values)

    def absorb(scores, near, values):
        masked = jnp.where(near, scores, neg_large)
        before = row_max[...]
        peak = jnp.maximum(before, jnp.max(masked, axis=1, keepdims=True))
        weights = jnp.where(near, jnp.exp(masked - peak), 0.0)
        scale = jnp.exp(before - peak)
        row_max[...] = peak
        row_total[...] = row_total[...] * scale + jnp.sum(weights, axis=1, keepdims=True)
        acc[...] = acc[...] * scale + jnp.dot(
            weights.astype(jnp.bfloat16), values, preferred_element_type=jnp.float32
        )

    def meet(zz, yy, half):
        def one(p, carry):
            arrived(zz, yy, 1 - core, half * group + p)
            return carry
        lax.fori_loop(0, group, one, 0)
        compute(zz, yy, half)

    def visited(distance, side, reach, origin):
        place = origin + jnp.where(side == 0, -distance, distance)
        inside = (distance >= 0) & (distance < reach) & (place >= 0) & (place < reach)
        return place, inside & jnp.logical_or(distance > 0, side == 0)

    def other_columns(body):
        if grid_fast == 2:
            body(1 - y)
            return
        def one(i, carry):
            yy, valid = visited(i // 2 + 1, lax.rem(i, 2), grid_fast, y)
            @pl.when(valid)
            def _():
                body(yy)
            return carry
        lax.fori_loop(0, 2 * (grid_fast - 1), one, 0)

    def along(zz, piece, side, act):
        each((2, 3, 0, 1, 4), (yes, yes, side == 1, side == 0, yes), zz, y, piece, False, act)

    def across(zz, yy, piece, act):
        each((2, 3, 4), (yy > y, yy < y, yes), zz, yy, piece, False, act)

    def receive(zz, yy, piece):
        arrived(zz, yy, core, piece)
        across(zz, yy, piece, start)

    farthest = jnp.where(2 * z >= grid_slow, 0, grid_slow - 1)

    def event(e, carry):
        distance = e // (2 * PIECES)
        piece = lax.rem(e // 2, PIECES)
        side = lax.rem(e, 2)
        half = piece // group

        @pl.when(e == 2 * PIECES * grid_slow)
        def _():
            for p in range(PIECES):
                each((2, 3, 0, 1, 4), (yes,) * 5, z, y, p, True, finish)

        zz, valid = visited(distance, side, grid_slow, z)
        @pl.when(valid & (distance > 0))
        def _():
            arrived(zz, y, core, piece)
            along(zz, piece, side, start)

        z1, valid1 = visited(distance - 1, side, grid_slow, z)
        z2, valid2 = visited(distance - 2, side, grid_slow, z)
        @pl.when(valid2)
        def _():
            other_columns(lambda yy: receive(z2, yy, piece))
            @pl.when(distance > 2)
            def _():
                along(z2, piece, side, finish)

        z3, valid3 = visited(distance - 3, side, grid_slow, z)
        @pl.when(valid3)
        def _():
            other_columns(lambda yy: across(z3, yy, piece, finish))

        near = valid1 & (lax.rem(piece, group) == 0)
        if grid_fast == 2:
            far = valid2 & (lax.rem(piece, group) == group - 1) & (z2 != farthest)
            @pl.when(near | far)
            def _():
                def one(i, carry):
                    @pl.when(jnp.where(i == 0, near, far))
                    def _():
                        meet(jnp.where(i == 0, z1, z2), jnp.where(i == 0, y, 1 - y), half)
                    return carry
                lax.fori_loop(0, 2, one, 0)
        else:
            @pl.when(near)
            def _():
                meet(z1, y, half)
            @pl.when(valid2 & (lax.rem(piece, group) == group - 1))
            def _():
                other_columns(lambda yy: meet(z2, yy, half))
        return carry

    lax.fori_loop(0, 2 * PIECES * (grid_slow + 2), event, 0)
    if grid_fast == 2:
        def last_pair(i, carry):
            cc = jnp.where(i == 0, core, 1 - core)
            @pl.when(i == 1)
            def _():
                for p in range(PIECES):
                    arrived(farthest, 1 - y, 1 - core, p)
            compute_core(farthest, 1 - y, cc)
            return carry
        lax.fori_loop(0, CORES, last_pair, 0)

    total = row_total[...]
    density = row_max[...] + jnp.log(total)
    dens_ref[...] = jnp.transpose(jnp.broadcast_to(density, (rows, rows)))[:1, :]
    mean_ref[...] = (acc[...] / total).astype(mean_ref.dtype)

    for e in range(2 * PIECES):
        last, valid = visited(grid_slow - 1, e % 2, grid_slow, z)
        @pl.when(valid)
        def _():
            other_columns(lambda yy: across(last, yy, e // 2, finish))


def per_device(device_count, embeddings, labels, row_slot):
    rows, width = embeddings.shape
    grid_slow, grid_fast = chip_grid(device_count)
    chips = device_count // CORES
    vmem = pl.BlockSpec(memory_space=pltpu.VMEM)
    density, mean = pl.pallas_call(
        functools.partial(kernel, grid_slow, grid_fast),
        out_shape=(
            pltpu.VMEM((1, rows), jnp.float32),
            pltpu.VMEM((rows, width), jnp.bfloat16),
        ),
        in_specs=[pl.BlockSpec(memory_space=pl.ANY), pl.BlockSpec(memory_space=pl.ANY)],
        out_specs=(vmem, vmem),
        scratch_shapes=[
            pltpu.VMEM((device_count * rows, width), jnp.bfloat16),
            pltpu.VMEM((device_count, 1, rows), jnp.int32),
            pltpu.VMEM((rows, width), jnp.bfloat16),
            pltpu.VMEM((rows, width), jnp.float32),
            pltpu.VMEM((rows, 1), jnp.float32),
            pltpu.VMEM((rows, 1), jnp.float32),
            pltpu.SemaphoreType.DMA((5, chips * PIECES)),
            pltpu.SemaphoreType.DMA((device_count * PIECES,)),
            pltpu.SemaphoreType.DMA((5, chips)),
            pltpu.SemaphoreType.DMA((device_count,)),
            pltpu.SemaphoreType.DMA((PIECES + 1,)),
            pltpu.SemaphoreType.DMA((1,)),
        ],
        compiler_params=pltpu.CompilerParams(collective_id=0, has_side_effects=True),
    )(embeddings, labels.reshape(1, rows))
    return density.reshape(rows), mean


def solution(mesh):
    return jax.shard_map(
        functools.partial(per_device, mesh.shape["docs"]),
        mesh=mesh,
        in_specs=(P(("groups", "docs"), None), P(("groups", "docs")), P(("groups", "docs"))),
        out_specs=(P(("groups", "docs")), P(("groups", "docs"), None)),
        check_vma=False,
    )
```

profile of v0, /device:TPU:0, one launch (start us, length us, event | category | flops | bytes accessed | tf_op | source)
XLA Modules:
  0.0 34.0 jit_solution(16629846970692178385)
XLA Ops:
  0.6 32.2 %shard_map.41 = (f32[1,128]{1,0:T(1,128)S(1)}, bf16[128,1024]{1,0:T(8,128)(2,1)S(1)}) custom-call(bf16[128,1024]{1,0:T(8,128)(2,1)} %x_ref.1, s32[1,128]{1,0:T(1,128)} %bitcast.3), custom_call_target="tpu_custom_call" | custom-call | tf_op jit(solution)/shard_map/pallas_call | solution.py:293
  32.8 0.5 %copy.6 = f32[128]{0:T(128)} copy(f32[128]{0:T(128)S(1)} %bitcast.2) | data formatting | bytes 1024
  33.3 0.7 %copy.7 = bf16[128,1024]{1,0:T(8,128)(2,1)} copy(bf16[128,1024]{1,0:T(8,128)(2,1)S(1)} %get-tuple-element.7) | data formatting | bytes 524288
where the time goes:
time: 34.3 us; the launch traced here: 34 us
  Pallas kernels  32.2 us (94%)
  local copies, waits for them, and re-layouts  1.22 us (4%)
  between operations  0.64 us (2%)
    pallas_call x1, Pallas kernels, per_device(): pl.pallas_call(functools.partial(kernel, grid_slow, grid_fast), out_shape...  32.2 us
    unnamed x2, local copies, waits for them, and re-layouts  1.22 us

commit v1 on v0

--- a/solution.py
+++ b/solution.py
@@ -12,6 +12,7 @@
 CORES = 2
 PIECES = 2
 HALVES = 1
+FOLDED_GRID = (4, 2)
 
 neg_large = -1e30
 kernel_gain = 4.0
@@ -285,12 +286,261 @@
             other_columns(lambda yy: across(last, yy, e // 2, finish))
 
 
-def per_device(device_count, embeddings, labels, row_slot):
-    rows, width = embeddings.shape
+def folded_kernel(
+    planes, x_ref, lab_ref, dens_ref, mean_ref,
+    buf, labs, acc, row_max, row_total,
+    send_sem, recv_sem, pair_sem, lsend_sem, lrecv_sem, own_sem,
+):
+    rows, width = x_ref.shape
+    half_rows = rows // 2
+    keys = CORES * rows
+    me = lax.axis_index("docs")
+    core = lax.rem(me, CORES)
+    y = lax.rem(me // CORES, 2)
+    z = me // (CORES * 2)
+    mirrored = 2 * z >= planes
+    end = (z == 0) | (z == planes - 1)
+    mid = jnp.logical_not(end)
+    home = jnp.where(end, 0, 1)
+
+    def chip(k, other):
+        zz = jnp.where(mirrored, planes - 1 - k, k)
+        return zz * 2 + (1 - y if other is True else y if other is False else jnp.where(other == 1, 1 - y, y))
+
+    def device(k, other, cc):
+        return chip(k, other) * CORES + cc
+
+    OUT, IN, SIDE, PAIR = range(4)
+    targets = (
+        device(0, False, core),
+        device(home + 1, False, core),
+        device(home, True, core),
+        device(home, False, 1 - core),
+    )
+
+    barrier = pltpu.get_barrier_semaphore()
+    for direction, target in enumerate(targets):
+        @pl.when((direction != OUT) | mid)
+        def _():
+            pl.semaphore_signal(barrier, inc=1, device_id={"docs": target}, device_id_type=MESH)
+
+    own_data = pltpu.make_async_copy(x_ref, buf.at[pl.ds(pl.multiple_of(me * rows, rows), rows)], own_sem.at[0])
+    own_data.start()
+    own_lab = pltpu.make_async_copy(lab_ref, labs.at[me], own_sem.at[1])
+    own_lab.start()
+    pl.semaphore_wait(barrier, jnp.where(mid, 4, 3))
+
+    def rows_of(slot, half):
+        if half is None:
+            return buf.at[pl.ds(pl.multiple_of(slot * rows, rows), rows)]
+        return buf.at[pl.ds(pl.multiple_of(slot * rows + half * half_rows, half_rows), half_rows)]
+
+    def data_copy(direction, k, other, half, own=False):
+        slot = device(k, other, core)
+        place = rows_of(slot, half)
+        if own:
+            source = x_ref if half is None else x_ref.at[pl.ds(half * half_rows, half_rows)]
+        else:
+            source = place
+        if direction == PAIR:
+            done = pair_sem.at[chip(k, other)]
+        else:
+            done = recv_sem.at[chip(k, other) * 2 + half]
+        return pltpu.make_async_remote_copy(
+            source, place, send_sem.at[direction], done,
+            device_id={"docs": targets[direction]}, device_id_type=MESH,
+        )
+
+    def lab_copy(direction, k, other, own=False):
+        slot = device(k, other, core)
+        return pltpu.make_async_remote_copy(
+            lab_ref if own else labs.at[slot], labs.at[slot],
+            lsend_sem.at[0], lrecv_sem.at[slot],
+            device_id={"docs": targets[direction]}, device_id_type=MESH,
+        )
+
+    def send(k, other, half, directions):
+        for direction in directions:
+            if half != 1:
+                lab_copy(direction, k, other).start()
+            data_copy(direction, k, other, half).start()
+
+    def arrived(k, other, half):
+        if half == 0:
+            lab_copy(SIDE, k, other).wait_recv()
+        data_copy(SIDE, k, other, half).wait_recv()
+
+    def pass_on(k, other, half, directions):
+        arrived(k, other, half)
+        send(k, other, half, directions)
+
+    for half in range(2):
+        for direction in (SIDE, OUT, IN):
+            def _():
+                if half == 0:
+                    lab_copy(direction, home, False, own=True).start()
+                data_copy(direction, home, False, half, own=True).start()
+            if direction == OUT:
+                pl.when(mid)(_)
+            else:
+                _()
+    lab_copy(PAIR, home, False, own=True).start()
+    data_copy(PAIR, home, False, None, own=True).start()
+
+    row_max[...] = jnp.full_like(row_max, neg_large)
+    row_total[...] = jnp.zeros_like(row_total)
+    acc[...] = jnp.zeros_like(acc)
+    own_lab.wait()
+    label_column = jnp.transpose(
+        jnp.broadcast_to(labs[me].astype(jnp.float32), (rows, rows))
+    )[:, :1]
+    gap = lax.broadcasted_iota(jnp.int32, (rows, keys), 1) - lax.broadcasted_iota(jnp.int32, (rows, keys), 0)
+    own_data.wait()
+
+    def pick(i, values):
+        return sum(jnp.where(i == j, value, 0) for j, value in enumerate(values) if value)
+
+    def step(i, carry):
+        k = jnp.where(end, pick(i, (0, 1, 0, 2, 1, 3, 2, 3)), pick(i, (1, 2, 0, 1, 3, 0, 2, 3)))
+        other = jnp.where(end, pick(i, (0, 0, 1, 0, 1, 0, 1, 1)), pick(i, (0, 0, 0, 1, 0, 1, 1, 1)))
+
+        @pl.when(end & (i == 1))
+        def _():
+            pass_on(1, False, 0, (SIDE,))
+            pass_on(0, True, 0, (IN,))
+            pass_on(1, False, 1, (SIDE,))
+            send(1, False, None, (PAIR,))
+            pass_on(0, True, 1, (IN,))
+            send(0, True, None, (PAIR,))
+
+        @pl.when(end & (i == 3))
+        def _():
+            pass_on(2, False, 0, (SIDE,))
+            pass_on(2, False, 1, (SIDE,))
+            send(2, False, None, (PAIR,))
+            arrived(1, True, 0)
+            arrived(1, True, 1)
+            send(1, True, None, (PAIR,))
+
+        @pl.when(end & (i == 5))
+        def _():
+            pass_on(3, False, 0, (SIDE,))
+            arrived(3, False, 1)
+            send(3, False, None, (PAIR,))
+            arrived(2, True, 0)
+            arrived(2, True, 1)
+            send(2, True, None, (PAIR,))
+
+        @pl.when(mid & (i == 1))
+        def _():
+            pass_on(2, False, 0, (OUT, SIDE))
+            pass_on(0, False, 0, (IN,))
+            pass_on(2, False, 1, (OUT, SIDE))
+            send(2, False, None, (PAIR,))
+            pass_on(0, False, 1, (IN,))
+            send(0, False, None, (PAIR,))
+            arrived(1, True, 0)
+            arrived(1, True, 1)
+            send(1, True, None, (PAIR,))
+
+        @pl.when(mid & (i == 3))
+        def _():
+            pass_on(3, False, 0, (OUT,))
+
+        @pl.when(mid & (i == 4))
+        def _():
+            pass_on(3, False, 1, (OUT, SIDE))
+            send(3, False, 0, (SIDE,))
+            send(3, False, None, (PAIR,))
+            arrived(0, True, 0)
+            arrived(0, True, 1)
+            send(0, True, None, (PAIR,))
+            arrived(2, True, 0)
+            arrived(2, True, 1)
+            send(2, True, None, (PAIR,))
+
+        @pl.when(i == 7)
+        def _():
+            arrived(3, True, 1)
+            @pl.when(mid)
+            def _():
+                send(3, True, 1, (OUT,))
+            send(3, True, 1, (PAIR,))
+            arrived(3, True, 0)
+            send(3, True, 0, (PAIR,))
+
+        where = chip(k, other)
+        theirs = where * CORES + 1 - core
+        pltpu.make_async_remote_copy(
+            labs.at[theirs], labs.at[theirs], lsend_sem.at[0], lrecv_sem.at[theirs],
+            device_id={"docs": targets[PAIR]}, device_id_type=MESH,
+        ).wait_recv()
+        pltpu.make_async_remote_copy(
+            rows_of(theirs, None), rows_of(theirs, None), send_sem.at[PAIR], pair_sem.at[where],
+            device_id={"docs": targets[PAIR]}, device_id_type=MESH,
+        ).wait_recv()
+
+        values = buf[pl.ds(pl.multiple_of(where * keys, keys), keys), :]
+        tags = jnp.concatenate([labs[where * CORES + cc].astype(jnp.float32) for cc in range(CORES)], axis=1)
+        mine = buf[pl.ds(pl.multiple_of(me * rows, rows), rows), :]
+        scores = lax.dot_general(
+            mine, values, (((1,), (1,)), ((), ())), preferred_element_type=jnp.float32
+        ) * (kernel_gain / math.sqrt(width))
+        near = (label_column == tags) & (gap != jnp.where(i == 0, core * rows, keys))
+        masked = jnp.where(near, scores, neg_large)
+        before = row_max[...]
+        peak = jnp.maximum(before, jnp.max(masked, axis=1, keepdims=True))
+        weights = jnp.where(near, jnp.exp(masked - peak), 0.0)
+        scale = jnp.exp(before - peak)
+        row_max[...] = peak
+        row_total[...] = row_total[...] * scale + jnp.sum(weights, axis=1, keepdims=True)
+        acc[...] = acc[...] * scale + jnp.dot(
+            weights.astype(jnp.bfloat16), values, preferred_element_type=jnp.float32
+        )
+        return carry
+
+    lax.fori_loop(0, 2 * planes, step, 0)
+
+    total = row_total[...]
+    density = row_max[...] + jnp.log(total)
+    dens_ref[...] = jnp.transpose(jnp.broadcast_to(density, (rows, rows)))[:1, :]
+    mean_ref[...] = (acc[...] / total).astype(mean_ref.dtype)
+
+    def sent(direction, halves):
+        amount = buf.at[pl.ds(0, halves * half_rows)]
+        pltpu.make_async_remote_copy(
+            amount, amount, send_sem.at[direction], pair_sem.at[0],
+            device_id={"docs": targets[direction]}, device_id_type=MESH,
+        ).wait_send()
+
+    def labs_sent(count):
+        amount = labs.at[pl.ds(0, count)]
+        pltpu.make_async_remote_copy(
+            amount, amount, lsend_sem.at[0], lrecv_sem.at[0],
+            device_id={"docs": targets[PAIR]}, device_id_type=MESH,
+        ).wait_send()
+
+    @pl.when(end)
+    def _():
+        sent(IN, 4)
+        sent(SIDE, 7)
+        sent(PAIR, 16)
+        labs_sent(14)
+
+    @pl.when(mid)
+    def _():
+        sent(OUT, 7)
+        sent(IN, 4)
+        sent(SIDE, 6)
+        sent(PAIR, 16)
+        labs_sent(16)
+
+
+def general_call(device_count, rows, width):
     grid_slow, grid_fast = chip_grid(device_count)
     chips = device_count // CORES
     vmem = pl.BlockSpec(memory_space=pltpu.VMEM)
-    density, mean = pl.pallas_call(
+    return pl.pallas_call(
         functools.partial(kernel, grid_slow, grid_fast),
         out_shape=(
             pltpu.VMEM((1, rows), jnp.float32),
@@ -313,7 +563,41 @@
             pltpu.SemaphoreType.DMA((1,)),
         ],
         compiler_params=pltpu.CompilerParams(collective_id=0, has_side_effects=True),
-    )(embeddings, labels.reshape(1, rows))
+    )
+
+
+def folded_call(device_count, rows, width):
+    chips = device_count // CORES
+    vmem = pl.BlockSpec(memory_space=pltpu.VMEM)
+    return pl.pallas_call(
+        functools.partial(folded_kernel, chips // 2),
+        out_shape=(
+            pltpu.VMEM((1, rows), jnp.float32),
+            pltpu.VMEM((rows, width), jnp.bfloat16),
+        ),
+        in_specs=[pl.BlockSpec(memory_space=pl.ANY), pl.BlockSpec(memory_space=pl.ANY)],
+        out_specs=(vmem, vmem),
+        scratch_shapes=[
+            pltpu.VMEM((device_count * rows, width), jnp.bfloat16),
+            pltpu.VMEM((device_count, 1, rows), jnp.int32),
+            pltpu.VMEM((rows, width), jnp.float32),
+            pltpu.VMEM((rows, 1), jnp.float32),
+            pltpu.VMEM((rows, 1), jnp.float32),
+            pltpu.SemaphoreType.DMA((4,)),
+            pltpu.SemaphoreType.DMA((2 * chips,)),
+            pltpu.SemaphoreType.DMA((chips,)),
+            pltpu.SemaphoreType.DMA((1,)),
+            pltpu.SemaphoreType.DMA((device_count,)),
+            pltpu.SemaphoreType.DMA((2,)),
+        ],
+        compiler_params=pltpu.CompilerParams(collective_id=0, has_side_effects=True),
+    )
+
+
+def per_device(device_count, embeddings, labels, row_slot):
+    rows, width = embeddings.shape
+    call = folded_call if chip_grid(device_count) == FOLDED_GRID else general_call
+    density, mean = call(device_count, rows, width)(embeddings, labels.reshape(1, rows))
     return density.reshape(rows), mean
 
 

time: 34.3 us -> 31.4 us (0.915)
  Pallas kernels: 32.2 us -> 29.3 us
    pallas_call x1, Pallas kernels: 32.2 us -> 29.3 us  [per_device(): call(device_count, rows, width)(embeddings, labels.reshape(1, rows))]
where the time goes in v1:
time: 31.4 us; the launch traced here: 31.1 us
  Pallas kernels  29.3 us (93%)
  local copies, waits for them, and re-layouts  1.22 us (4%)
  between operations  0.64 us (2%)
    pallas_call x1, Pallas kernels, per_device(): call(device_count, rows, width)(embeddings, labels.reshape(1, rows))  29.3 us
    unnamed x2, local copies, waits for them, and re-layouts  1.22 us

profile of v1, /device:TPU:0, one launch (start us, length us, event | category | flops | bytes accessed | tf_op | source)
XLA Modules:
  0.0 31.1 jit_solution(12312810797888162029)
XLA Ops:
  0.6 29.3 %shard_map.41 = (f32[1,128]{1,0:T(1,128)S(1)}, bf16[128,1024]{1,0:T(8,128)(2,1)S(1)}) custom-call(bf16[128,1024]{1,0:T(8,128)(2,1)} %x_ref.1, s32[1,128]{1,0:T(1,128)} %bitcast.3), custom_call_target="tpu_custom_call" | custom-call | tf_op jit(solution)/shard_map/pallas_call | solution.py:600
  29.9 0.5 %copy.6 = f32[128]{0:T(128)} copy(f32[128]{0:T(128)S(1)} %bitcast.2) | data formatting | bytes 1024
  30.4 0.7 %copy.7 = bf16[128,1024]{1,0:T(8,128)(2,1)} copy(bf16[128,1024]{1,0:T(8,128)(2,1)S(1)} %get-tuple-element.7) | data formatting | bytes 524288

commit v2 on v1

--- a/solution.py
+++ b/solution.py
@@ -289,7 +289,7 @@
 def folded_kernel(
     planes, x_ref, lab_ref, dens_ref, mean_ref,
     buf, labs, acc, row_max, row_total,
-    send_sem, recv_sem, pair_sem, lsend_sem, lrecv_sem, own_sem,
+    send_sem, recv_sem, pair_sem, lsend_sem, lrecv_sem, own_sem, ready_sem,
 ):
     rows, width = x_ref.shape
     half_rows = rows // 2
@@ -311,6 +311,7 @@
         return chip(k, other) * CORES + cc
 
     OUT, IN, SIDE, PAIR = range(4)
+    AXIS = (0, 0, 1, 2)
     targets = (
         device(0, False, core),
         device(home + 1, False, core),
@@ -318,9 +319,11 @@
         device(home, False, 1 - core),
     )
 
+    up = (mid & mirrored, jnp.logical_not(mirrored), y == 0, core == 0)
+    down = (mid & jnp.logical_not(mirrored), mirrored, y == 1, core == 1)
     barrier = pltpu.get_barrier_semaphore()
-    for direction, target in enumerate(targets):
-        @pl.when((direction != OUT) | mid)
+    for target, higher in zip(targets, up):
+        @pl.when(higher)
         def _():
             pl.semaphore_signal(barrier, inc=1, device_id={"docs": target}, device_id_type=MESH)
 
@@ -328,7 +331,17 @@
     own_data.start()
     own_lab = pltpu.make_async_copy(lab_ref, labs.at[me], own_sem.at[1])
     own_lab.start()
-    pl.semaphore_wait(barrier, jnp.where(mid, 4, 3))
+    lower_count = sum(lower.astype(jnp.int32) for lower in down)
+    @pl.when(lower_count > 0)
+    def _():
+        pl.semaphore_wait(barrier, lower_count)
+    for direction, lower in enumerate(down):
+        @pl.when(lower)
+        def _():
+            pl.semaphore_signal(
+                ready_sem.at[AXIS[direction]], inc=1,
+                device_id={"docs": targets[direction]}, device_id_type=MESH,
+            )
 
     def rows_of(slot, half):
         if half is None:
@@ -374,18 +387,20 @@
         arrived(k, other, half)
         send(k, other, half, directions)
 
-    for half in range(2):
-        for direction in (SIDE, OUT, IN):
-            def _():
-                if half == 0:
-                    lab_copy(direction, home, False, own=True).start()
-                data_copy(direction, home, False, half, own=True).start()
-            if direction == OUT:
-                pl.when(mid)(_)
-            else:
-                _()
-    lab_copy(PAIR, home, False, own=True).start()
-    data_copy(PAIR, home, False, None, own=True).start()
+    def start_own(direction):
+        lab_copy(direction, home, False, own=True).start()
+        for half in {SIDE: (1, 0), PAIR: (None,)}.get(direction, (0, 1)):
+            data_copy(direction, home, False, half, own=True).start()
+
+    for direction, lower in enumerate(down):
+        @pl.when(lower)
+        def _():
+            start_own(direction)
+    for direction, higher in reversed(tuple(enumerate(up))):
+        @pl.when(higher)
+        def _():
+            pl.semaphore_wait(ready_sem.at[AXIS[direction]], 1)
+            start_own(direction)
 
     row_max[...] = jnp.full_like(row_max, neg_large)
     row_total[...] = jnp.zeros_like(row_total)
@@ -407,10 +422,10 @@
         @pl.when(end & (i == 1))
         def _():
             pass_on(1, False, 0, (SIDE,))
-            pass_on(0, True, 0, (IN,))
+            pass_on(0, True, 1, (IN,))
             pass_on(1, False, 1, (SIDE,))
             send(1, False, None, (PAIR,))
-            pass_on(0, True, 1, (IN,))
+            pass_on(0, True, 0, (IN,))
             send(0, True, None, (PAIR,))
 
         @pl.when(end & (i == 3))
@@ -445,15 +460,14 @@
 
         @pl.when(mid & (i == 3))
         def _():
-            pass_on(3, False, 0, (OUT,))
+            pass_on(3, False, 0, (OUT, SIDE))
+            pass_on(0, True, 1, (IN,))
 
         @pl.when(mid & (i == 4))
         def _():
-            pass_on(3, False, 1, (OUT, SIDE))
-            send(3, False, 0, (SIDE,))
+            pass_on(3, False, 1, (OUT,))
             send(3, False, None, (PAIR,))
             arrived(0, True, 0)
-            arrived(0, True, 1)
             send(0, True, None, (PAIR,))
             arrived(2, True, 0)
             arrived(2, True, 1)
@@ -530,8 +544,8 @@
     @pl.when(mid)
     def _():
         sent(OUT, 7)
-        sent(IN, 4)
-        sent(SIDE, 6)
+        sent(IN, 5)
+        sent(SIDE, 5)
         sent(PAIR, 16)
         labs_sent(16)
 
@@ -589,6 +603,7 @@
             pltpu.SemaphoreType.DMA((1,)),
             pltpu.SemaphoreType.DMA((device_count,)),
             pltpu.SemaphoreType.DMA((2,)),
+            pltpu.SemaphoreType.REGULAR((3,)),
         ],
         compiler_params=pltpu.CompilerParams(collective_id=0, has_side_effects=True),
     )

time: 31.4 us -> 30 us (0.955)
  Pallas kernels: 29.3 us -> 28 us
    pallas_call x1, Pallas kernels: 29.3 us -> 28 us  [per_device(): call(device_count, rows, width)(embeddings, labels.reshape(1, rows))]
where the time goes in v2:
time: 30 us; the launch traced here: 29.9 us
  Pallas kernels  28 us (93%)
  local copies, waits for them, and re-layouts  1.22 us (4%)
  between operations  0.64 us (2%)
    pallas_call x1, Pallas kernels, per_device(): call(device_count, rows, width)(embeddings, labels.reshape(1, rows))  28 us
    unnamed x2, local copies, waits for them, and re-layouts  1.22 us

profile of v2, /device:TPU:0, one launch (start us, length us, event | category | flops | bytes accessed | tf_op | source)
XLA Modules:
  0.0 29.9 jit_solution(151880625980530172)
XLA Ops:
  0.6 28.0 %shard_map.41 = (f32[1,128]{1,0:T(1,128)S(1)}, bf16[128,1024]{1,0:T(8,128)(2,1)S(1)}) custom-call(bf16[128,1024]{1,0:T(8,128)(2,1)} %x_ref.1, s32[1,128]{1,0:T(1,128)} %bitcast.3), custom_call_target="tpu_custom_call" | custom-call | tf_op jit(solution)/shard_map/pallas_call | solution.py:615
  28.6 0.5 %copy.6 = f32[128]{0:T(128)} copy(f32[128]{0:T(128)S(1)} %bitcast.2) | data formatting | bytes 1024
  29.2 0.7 %copy.7 = bf16[128,1024]{1,0:T(8,128)(2,1)} copy(bf16[128,1024]{1,0:T(8,128)(2,1)S(1)} %get-tuple-element.7) | data formatting | bytes 524288

commit v3 on v2

--- a/solution.py
+++ b/solution.py
@@ -15,6 +15,7 @@
 FOLDED_GRID = (4, 2)
 
 neg_large = -1e30
+neg_start = -1e29
 kernel_gain = 4.0
 
 
@@ -293,7 +294,6 @@
 ):
     rows, width = x_ref.shape
     half_rows = rows // 2
-    keys = CORES * rows
     me = lax.axis_index("docs")
     core = lax.rem(me, CORES)
     y = lax.rem(me // CORES, 2)
@@ -301,23 +301,22 @@
     mirrored = 2 * z >= planes
     end = (z == 0) | (z == planes - 1)
     mid = jnp.logical_not(end)
-    home = jnp.where(end, 0, 1)
-
-    def chip(k, other):
+
+    def device(k, column, cc):
         zz = jnp.where(mirrored, planes - 1 - k, k)
-        return zz * 2 + (1 - y if other is True else y if other is False else jnp.where(other == 1, 1 - y, y))
-
-    def device(k, other, cc):
-        return chip(k, other) * CORES + cc
+        return (zz * 2 + column) * CORES + cc
 
     OUT, IN, SIDE, PAIR = range(4)
     AXIS = (0, 0, 1, 2)
+    home = jnp.where(end, 0, 1)
     targets = (
-        device(0, False, core),
-        device(home + 1, False, core),
-        device(home, True, core),
-        device(home, False, 1 - core),
+        device(0, y, core),
+        device(home + 1, y, core),
+        device(home, 1 - y, core),
+        device(home, y, 1 - core),
     )
+    END_ORDER = ((0, 0), (1, 0), (0, 1), (2, 0), (1, 1), (3, 0), (2, 1), (3, 1))
+    MID_ORDER = ((1, 0), (2, 0), (0, 0), (3, 0), (0, 1), (1, 1), (2, 1), (3, 1))
 
     up = (mid & mirrored, jnp.logical_not(mirrored), y == 0, core == 0)
     down = (mid & jnp.logical_not(mirrored), mirrored, y == 1, core == 1)
@@ -327,9 +326,15 @@
         def _():
             pl.semaphore_signal(barrier, inc=1, device_id={"docs": target}, device_id_type=MESH)
 
-    own_data = pltpu.make_async_copy(x_ref, buf.at[pl.ds(pl.multiple_of(me * rows, rows), rows)], own_sem.at[0])
+    def rows_of(slot, cc, half):
+        first = (slot * CORES + cc) * rows
+        if half is None:
+            return buf.at[pl.ds(pl.multiple_of(first, rows), rows)]
+        return buf.at[pl.ds(pl.multiple_of(first + half * half_rows, half_rows), half_rows)]
+
+    own_data = pltpu.make_async_copy(x_ref, rows_of(0, core, None), own_sem.at[0])
     own_data.start()
-    own_lab = pltpu.make_async_copy(lab_ref, labs.at[me], own_sem.at[1])
+    own_lab = pltpu.make_async_copy(lab_ref, labs.at[core], own_sem.at[1])
     own_lab.start()
     lower_count = sum(lower.astype(jnp.int32) for lower in down)
     @pl.when(lower_count > 0)
@@ -343,54 +348,82 @@
                 device_id={"docs": targets[direction]}, device_id_type=MESH,
             )
 
-    def rows_of(slot, half):
-        if half is None:
-            return buf.at[pl.ds(pl.multiple_of(slot * rows, rows), rows)]
-        return buf.at[pl.ds(pl.multiple_of(slot * rows + half * half_rows, half_rows), half_rows)]
-
-    def data_copy(direction, k, other, half, own=False):
-        slot = device(k, other, core)
-        place = rows_of(slot, half)
-        if own:
+    def data_copy(direction, slot, there, half, own=False):
+        if not own:
+            source = rows_of(slot, core, half)
+        else:
             source = x_ref if half is None else x_ref.at[pl.ds(half * half_rows, half_rows)]
-        else:
-            source = place
-        if direction == PAIR:
-            done = pair_sem.at[chip(k, other)]
-        else:
-            done = recv_sem.at[chip(k, other) * 2 + half]
+        done = pair_sem.at[there] if direction == PAIR else recv_sem.at[there * 2 + half]
         return pltpu.make_async_remote_copy(
-            source, place, send_sem.at[direction], done,
+            source, rows_of(there, core, half), send_sem.at[direction], done,
             device_id={"docs": targets[direction]}, device_id_type=MESH,
         )
 
-    def lab_copy(direction, k, other, own=False):
-        slot = device(k, other, core)
+    def lab_copy(direction, slot, there, own=False):
+        there = there * CORES + core
         return pltpu.make_async_remote_copy(
-            lab_ref if own else labs.at[slot], labs.at[slot],
-            lsend_sem.at[0], lrecv_sem.at[slot],
+            lab_ref if own else labs.at[slot * CORES + core], labs.at[there],
+            lsend_sem.at[0], lrecv_sem.at[there],
             device_id={"docs": targets[direction]}, device_id_type=MESH,
         )
 
-    def send(k, other, half, directions):
-        for direction in directions:
-            if half != 1:
-                lab_copy(direction, k, other).start()
-            data_copy(direction, k, other, half).start()
-
-    def arrived(k, other, half):
-        if half == 0:
-            lab_copy(SIDE, k, other).wait_recv()
-        data_copy(SIDE, k, other, half).wait_recv()
-
-    def pass_on(k, other, half, directions):
-        arrived(k, other, half)
-        send(k, other, half, directions)
+    class Role:
+        def __init__(self, is_end):
+            self.is_end = is_end
+            self.order = END_ORDER if is_end else MID_ORDER
+
+        def slot(self, k, other):
+            return self.order.index((k, other))
+
+        def there(self, direction, k, other):
+            if direction == SIDE:
+                return self.slot(k, 1 - other)
+            if direction == PAIR:
+                return self.slot(k, other)
+            if direction == OUT:
+                return END_ORDER.index((k, other))
+            return MID_ORDER.index((k if self.is_end else planes - 1 - k, other))
+
+        def send(self, k, other, half, directions, own=False):
+            for direction in directions:
+                slot, there = self.slot(k, other), self.there(direction, k, other)
+                if half != 1:
+                    lab_copy(direction, slot, there, own).start()
+                data_copy(direction, slot, there, half, own).start()
+
+        def arrived(self, k, other, half):
+            slot = self.slot(k, other)
+            if half == 0:
+                lab_copy(SIDE, slot, slot).wait_recv()
+            data_copy(SIDE, slot, slot, half).wait_recv()
+
+        def pass_on(self, k, other, half, directions):
+            self.arrived(k, other, half)
+            self.send(k, other, half, directions)
+
+        def pair(self, k, other):
+            self.send(k, other, None, (PAIR,))
+
+        def gather(self, k, other):
+            self.arrived(k, other, 1)
+            self.arrived(k, other, 0)
+            self.pair(k, other)
+
+    at_end, at_mid = Role(True), Role(False)
 
     def start_own(direction):
-        lab_copy(direction, home, False, own=True).start()
-        for half in {SIDE: (1, 0), PAIR: (None,)}.get(direction, (0, 1)):
-            data_copy(direction, home, False, half, own=True).start()
+        def by(role):
+            k = 0 if role.is_end else 1
+            for half in {SIDE: (1, 0), PAIR: (None,)}.get(direction, (0, 1)):
+                role.send(k, 0, half, (direction,), own=True)
+
+        if direction == OUT:
+            by(at_mid)
+        elif direction == PAIR:
+            by(at_end)
+        else:
+            pl.when(end)(lambda: by(at_end))
+            pl.when(mid)(lambda: by(at_mid))
 
     for direction, lower in enumerate(down):
         @pl.when(lower)
@@ -402,123 +435,138 @@
             pl.semaphore_wait(ready_sem.at[AXIS[direction]], 1)
             start_own(direction)
 
-    row_max[...] = jnp.full_like(row_max, neg_large)
-    row_total[...] = jnp.zeros_like(row_total)
-    acc[...] = jnp.zeros_like(acc)
     own_lab.wait()
     label_column = jnp.transpose(
-        jnp.broadcast_to(labs[me].astype(jnp.float32), (rows, rows))
+        jnp.broadcast_to(labs[core].astype(jnp.float32), (rows, rows))
     )[:, :1]
-    gap = lax.broadcasted_iota(jnp.int32, (rows, keys), 1) - lax.broadcasted_iota(jnp.int32, (rows, keys), 0)
     own_data.wait()
 
-    def pick(i, values):
-        return sum(jnp.where(i == j, value, 0) for j, value in enumerate(values) if value)
-
-    def step(i, carry):
-        k = jnp.where(end, pick(i, (0, 1, 0, 2, 1, 3, 2, 3)), pick(i, (1, 2, 0, 1, 3, 0, 2, 3)))
-        other = jnp.where(end, pick(i, (0, 0, 1, 0, 1, 0, 1, 1)), pick(i, (0, 0, 0, 1, 0, 1, 1, 1)))
-
-        @pl.when(end & (i == 1))
-        def _():
-            pass_on(1, False, 0, (SIDE,))
-            pass_on(0, True, 1, (IN,))
-            pass_on(1, False, 1, (SIDE,))
-            send(1, False, None, (PAIR,))
-            pass_on(0, True, 0, (IN,))
-            send(0, True, None, (PAIR,))
-
-        @pl.when(end & (i == 3))
-        def _():
-            pass_on(2, False, 0, (SIDE,))
-            pass_on(2, False, 1, (SIDE,))
-            send(2, False, None, (PAIR,))
-            arrived(1, True, 0)
-            arrived(1, True, 1)
-            send(1, True, None, (PAIR,))
-
-        @pl.when(end & (i == 5))
-        def _():
-            pass_on(3, False, 0, (SIDE,))
-            arrived(3, False, 1)
-            send(3, False, None, (PAIR,))
-            arrived(2, True, 0)
-            arrived(2, True, 1)
-            send(2, True, None, (PAIR,))
-
-        @pl.when(mid & (i == 1))
-        def _():
-            pass_on(2, False, 0, (OUT, SIDE))
-            pass_on(0, False, 0, (IN,))
-            pass_on(2, False, 1, (OUT, SIDE))
-            send(2, False, None, (PAIR,))
-            pass_on(0, False, 1, (IN,))
-            send(0, False, None, (PAIR,))
-            arrived(1, True, 0)
-            arrived(1, True, 1)
-            send(1, True, None, (PAIR,))
-
-        @pl.when(mid & (i == 3))
-        def _():
-            pass_on(3, False, 0, (OUT, SIDE))
-            pass_on(0, True, 1, (IN,))
-
-        @pl.when(mid & (i == 4))
-        def _():
-            pass_on(3, False, 1, (OUT,))
-            send(3, False, None, (PAIR,))
-            arrived(0, True, 0)
-            send(0, True, None, (PAIR,))
-            arrived(2, True, 0)
-            arrived(2, True, 1)
-            send(2, True, None, (PAIR,))
-
-        @pl.when(i == 7)
-        def _():
-            arrived(3, True, 1)
-            @pl.when(mid)
-            def _():
-                send(3, True, 1, (OUT,))
-            send(3, True, 1, (PAIR,))
-            arrived(3, True, 0)
-            send(3, True, 0, (PAIR,))
-
-        where = chip(k, other)
-        theirs = where * CORES + 1 - core
+    def from_pair(slot):
+        theirs = slot * CORES + 1 - core
         pltpu.make_async_remote_copy(
             labs.at[theirs], labs.at[theirs], lsend_sem.at[0], lrecv_sem.at[theirs],
             device_id={"docs": targets[PAIR]}, device_id_type=MESH,
         ).wait_recv()
+        place = rows_of(slot, 1 - core, None)
         pltpu.make_async_remote_copy(
-            rows_of(theirs, None), rows_of(theirs, None), send_sem.at[PAIR], pair_sem.at[where],
+            place, place, send_sem.at[PAIR], pair_sem.at[slot],
             device_id={"docs": targets[PAIR]}, device_id_type=MESH,
         ).wait_recv()
 
-        values = buf[pl.ds(pl.multiple_of(where * keys, keys), keys), :]
-        tags = jnp.concatenate([labs[where * CORES + cc].astype(jnp.float32) for cc in range(CORES)], axis=1)
-        mine = buf[pl.ds(pl.multiple_of(me * rows, rows), rows), :]
+    def masked_scores(slot, count):
+        keys = count * CORES * rows
+        values = buf[pl.ds(pl.multiple_of(slot * CORES * rows, rows), keys), :]
+        mine = buf[pl.ds(pl.multiple_of(core * rows, rows), rows), :]
+        tags = jnp.concatenate(
+            [labs[slot * CORES + n].astype(jnp.float32) for n in range(count * CORES)], axis=1
+        )
         scores = lax.dot_general(
             mine, values, (((1,), (1,)), ((), ())), preferred_element_type=jnp.float32
         ) * (kernel_gain / math.sqrt(width))
-        near = (label_column == tags) & (gap != jnp.where(i == 0, core * rows, keys))
+        return scores, label_column == tags, values
+
+    def first_block():
+        scores, near, values = masked_scores(0, 1)
+        gap = lax.broadcasted_iota(jnp.int32, near.shape, 1) - lax.broadcasted_iota(jnp.int32, near.shape, 0)
+        masked = jnp.where(near & (gap != core * rows), scores, neg_large)
+        peak = jnp.maximum(jnp.max(masked, axis=1, keepdims=True), neg_start)
+        weights = jnp.exp(masked - peak)
+        row_max[...] = peak
+        row_total[...] = jnp.sum(weights, axis=1, keepdims=True)
+        acc[...] = jnp.dot(weights.astype(jnp.bfloat16), values, preferred_element_type=jnp.float32)
+
+    def absorb(slot, count):
+        scores, near, values = masked_scores(slot, count)
         masked = jnp.where(near, scores, neg_large)
         before = row_max[...]
         peak = jnp.maximum(before, jnp.max(masked, axis=1, keepdims=True))
-        weights = jnp.where(near, jnp.exp(masked - peak), 0.0)
+        weights = jnp.exp(masked - peak)
         scale = jnp.exp(before - peak)
+        total = row_total[...] * scale + jnp.sum(weights, axis=1, keepdims=True)
+        gained = jnp.dot(weights.astype(jnp.bfloat16), values, preferred_element_type=jnp.float32)
+        return peak, total, scale, gained
+
+    from_pair(0)
+    first_block()
+
+    def step(j, carry):
+        @pl.when(end & (j == 1))
+        def _():
+            r = at_end
+            r.pass_on(1, 0, 0, (SIDE,))
+            r.pass_on(0, 1, 1, (IN,))
+            r.pass_on(1, 0, 1, (SIDE,))
+            r.pair(1, 0)
+            r.pass_on(0, 1, 0, (IN,))
+            r.pair(0, 1)
+            r.pass_on(2, 0, 0, (SIDE,))
+
+        @pl.when(end & (j == 2))
+        def _():
+            r = at_end
+            r.pass_on(2, 0, 1, (SIDE,))
+            r.pair(2, 0)
+            r.gather(1, 1)
+            r.pass_on(3, 0, 0, (SIDE,))
+
+        @pl.when(end & (j == 3))
+        def _():
+            r = at_end
+            r.arrived(3, 0, 1)
+            r.pair(3, 0)
+            r.gather(2, 1)
+
+        @pl.when(mid & (j == 1))
+        def _():
+            r = at_mid
+            r.pass_on(2, 0, 0, (OUT, SIDE))
+            r.pass_on(0, 0, 0, (IN,))
+            r.pass_on(2, 0, 1, (OUT, SIDE))
+            r.pair(2, 0)
+            r.pass_on(0, 0, 1, (IN,))
+            r.pair(0, 0)
+            r.gather(1, 1)
+            r.pass_on(3, 0, 0, (OUT, SIDE))
+            r.pass_on(0, 1, 1, (IN,))
+
+        @pl.when(mid & (j == 2))
+        def _():
+            r = at_mid
+            r.pass_on(3, 0, 1, (OUT,))
+            r.pair(3, 0)
+            r.arrived(0, 1, 0)
+            r.pair(0, 1)
+            r.gather(2, 1)
+
+        @pl.when(mid & (j == 3))
+        def _():
+            at_mid.pass_on(3, 1, 1, (OUT,))
+
+        slot = 2 * j - 1
+        from_pair(slot)
+        from_pair(slot + 1)
+        peak, total, scale, gained = absorb(slot, 2)
         row_max[...] = peak
-        row_total[...] = row_total[...] * scale + jnp.sum(weights, axis=1, keepdims=True)
-        acc[...] = acc[...] * scale + jnp.dot(
-            weights.astype(jnp.bfloat16), values, preferred_element_type=jnp.float32
-        )
+        row_total[...] = total
+        acc[...] = acc[...] * scale + gained
         return carry
 
-    lax.fori_loop(0, 2 * planes, step, 0)
-
-    total = row_total[...]
-    density = row_max[...] + jnp.log(total)
+    lax.fori_loop(1, planes, step, 0)
+
+    @pl.when(end)
+    def _():
+        at_end.arrived(3, 1, 1)
+
+    last = at_end
+    last.send(3, 1, 1, (PAIR,))
+    last.arrived(3, 1, 0)
+    last.send(3, 1, 0, (PAIR,))
+    from_pair(last.slot(3, 1))
+    peak, total, scale, gained = absorb(last.slot(3, 1), 1)
+    density = peak + jnp.log(total)
     dens_ref[...] = jnp.transpose(jnp.broadcast_to(density, (rows, rows)))[:1, :]
-    mean_ref[...] = (acc[...] / total).astype(mean_ref.dtype)
+    inverse = 1.0 / total
+    mean_ref[...] = ((acc[...] * scale + gained) * inverse).astype(mean_ref.dtype)
 
     def sent(direction, halves):
         amount = buf.at[pl.ds(0, halves * half_rows)]
@@ -548,6 +596,28 @@
         sent(SIDE, 5)
         sent(PAIR, 16)
         labs_sent(16)
+
+
+def publish_kernel(dens_ref, mean_ref, dens_out, mean_out, sem):
+    copies = (
+        pltpu.make_async_copy(mean_ref, mean_out, sem.at[0]),
+        pltpu.make_async_copy(dens_ref, dens_out, sem.at[1]),
+    )
+    for copy in copies:
+        copy.start()
+    for copy in copies:
+        copy.wait()
+
+
+def publish(density, mean):
+    held = [pltpu.with_memory_space_constraint(a, pltpu.VMEM) for a in (density, mean)]
+    return pl.pallas_call(
+        publish_kernel,
+        out_shape=tuple(jax.ShapeDtypeStruct(a.shape, a.dtype) for a in (density, mean)),
+        in_specs=[pl.BlockSpec(memory_space=pltpu.VMEM)] * 2,
+        out_specs=(pl.BlockSpec(memory_space=pltpu.HBM),) * 2,
+        scratch_shapes=[pltpu.SemaphoreType.DMA((2,))],
+    )(*held)
 
 
 def general_call(device_count, rows, width):
@@ -613,6 +683,7 @@
     rows, width = embeddings.shape
     call = folded_call if chip_grid(device_count) == FOLDED_GRID else general_call
     density, mean = call(device_count, rows, width)(embeddings, labels.reshape(1, rows))
+    density, mean = publish(density, mean)
     return density.reshape(rows), mean
 
 

time: 30 us -> 29 us (0.967)
  local copies, waits for them, and re-layouts: 1.22 us -> 0 us
    unnamed x2 -> x0, local copies, waits for them, and re-layouts: 1.22 us -> none
    pallas_call x0 -> x1, Pallas kernels: none -> 0.72 us  [publish(): pl.pallas_call(publish_kernel, out_shape=tuple((jax.ShapeDtypeStruct(a.sh...]
    pallas_call x1, Pallas kernels: 28 us -> 27.5 us  [per_device(): call(device_count, rows, width)(embeddings, labels.reshape(1, rows))]
where the time goes in v3:
time: 29 us; the launch traced here: 28.8 us
  Pallas kernels  28.2 us (97%)
  between operations  0.64 us (2%)
    pallas_call x1, Pallas kernels, per_device(): call(device_count, rows, width)(embeddings, labels.reshape(1, rows))  27.5 us
    pallas_call x1, Pallas kernels, publish(): pl.pallas_call(publish_kernel, out_shape=tuple((jax.ShapeDtypeStruct(a.sh...  0.72 us

profile of v3, /device:TPU:0, one launch (start us, length us, event | category | flops | bytes accessed | tf_op | source)
XLA Modules:
  0.0 28.8 jit_solution(4947291049250327602)
XLA Ops:
  0.6 27.5 %shard_map.41 = (f32[1,128]{1,0:T(1,128)S(1)}, bf16[128,1024]{1,0:T(8,128)(2,1)S(1)}) custom-call(bf16[128,1024]{1,0:T(8,128)(2,1)} %x_ref.1, s32[1,128]{1,0:T(1,128)} %bitcast.2), custom_call_target="tpu_custom_call" | custom-call | tf_op jit(solution)/shard_map/pallas_call | solution.py:685
  28.1 0.7 %shard_map.42 = (f32[1,128]{1,0:T(1,128)}, bf16[128,1024]{1,0:T(8,128)(2,1)}) custom-call(f32[1,128]{1,0:T(1,128)S(1)} %get-tuple-element.6.dens_ref, bf16[128,1024]{1,0:T(8,128)(2,1)S(1)} %get-tuple-element.7.mean_ref), custom_call_target="tpu_custom_call" | custom-call | tf_op jit(solution)/shard_map/pallas_call | solution.py:614

commit v4 on v3

--- a/solution.py
+++ b/solution.py
@@ -489,6 +489,8 @@
     from_pair(0)
     first_block()
 
+    last = at_end
+
     def step(j, carry):
         @pl.when(end & (j == 1))
         def _():
@@ -542,6 +544,16 @@
         def _():
             at_mid.pass_on(3, 1, 1, (OUT,))
 
+        @pl.when(j == planes - 1)
+        def _():
+            @pl.when(end)
+            def _():
+                at_end.arrived(3, 1, 1)
+
+            last.send(3, 1, 1, (PAIR,))
+            last.arrived(3, 1, 0)
+            last.send(3, 1, 0, (PAIR,))
+
         slot = 2 * j - 1
         from_pair(slot)
         from_pair(slot + 1)
@@ -553,14 +565,6 @@
 
     lax.fori_loop(1, planes, step, 0)
 
-    @pl.when(end)
-    def _():
-        at_end.arrived(3, 1, 1)
-
-    last = at_end
-    last.send(3, 1, 1, (PAIR,))
-    last.arrived(3, 1, 0)
-    last.send(3, 1, 0, (PAIR,))
     from_pair(last.slot(3, 1))
     peak, total, scale, gained = absorb(last.slot(3, 1), 1)
     density = peak + jnp.log(total)

time: 29 us -> 28.4 us (0.979)
  Pallas kernels: 28.2 us -> 27.6 us
    pallas_call x1, Pallas kernels: 27.5 us -> 26.9 us  [per_device(): call(device_count, rows, width)(embeddings, labels.reshape(1, rows))]
where the time goes in v4:
time: 28.4 us; the launch traced here: 28.3 us
  Pallas kernels  27.6 us (97%)
  between operations  0.64 us (2%)
    pallas_call x1, Pallas kernels, per_device(): call(device_count, rows, width)(embeddings, labels.reshape(1, rows))  26.9 us
    pallas_call x1, Pallas kernels, publish(): pl.pallas_call(publish_kernel, out_shape=tuple((jax.ShapeDtypeStruct(a.sh...  0.72 us

profile of v4, /device:TPU:0, one launch (start us, length us, event | category | flops | bytes accessed | tf_op | source)
XLA Modules:
  0.0 28.3 jit_solution(231143016277439701)
XLA Ops:
  0.6 26.9 %shard_map.41 = (f32[1,128]{1,0:T(1,128)S(1)}, bf16[128,1024]{1,0:T(8,128)(2,1)S(1)}) custom-call(bf16[128,1024]{1,0:T(8,128)(2,1)} %x_ref.1, s32[1,128]{1,0:T(1,128)} %bitcast.2), custom_call_target="tpu_custom_call" | custom-call | tf_op jit(solution)/shard_map/pallas_call | solution.py:689
  27.5 0.7 %shard_map.42 = (f32[1,128]{1,0:T(1,128)}, bf16[128,1024]{1,0:T(8,128)(2,1)}) custom-call(f32[1,128]{1,0:T(1,128)S(1)} %get-tuple-element.6.dens_ref, bf16[128,1024]{1,0:T(8,128)(2,1)S(1)} %get-tuple-element.7.mean_ref), custom_call_target="tpu_custom_call" | custom-call | tf_op jit(solution)/shard_map/pallas_call | solution.py:618

commit v5 on v3

--- a/solution.py
+++ b/solution.py
@@ -289,11 +289,17 @@
 
 def folded_kernel(
     planes, x_ref, lab_ref, dens_ref, mean_ref,
-    buf, labs, acc, row_max, row_total,
-    send_sem, recv_sem, pair_sem, lsend_sem, lrecv_sem, own_sem, ready_sem,
+    buf, labs, meter, acc, row_max, row_total,
+    send_sem, lsend_sem, recv_sem, pair_sem, own_sem, ready_sem,
 ):
     rows, width = x_ref.shape
+    row_units = width * x_ref.dtype.itemsize // (rows * lab_ref.dtype.itemsize)
     half_rows = rows // 2
+    tip = rows // 8
+    FIRST, SECOND, WHOLE = (0, half_rows), (half_rows, half_rows), (0, rows)
+    FIRST_BODY, FIRST_TIP = (0, half_rows - tip), (half_rows - tip, tip)
+    SECOND_TIP, SECOND_BODY = (half_rows, tip), (half_rows + tip, half_rows - tip)
+    TIPS = (half_rows - tip, 2 * tip)
     me = lax.axis_index("docs")
     core = lax.rem(me, CORES)
     y = lax.rem(me // CORES, 2)
@@ -326,46 +332,36 @@
         def _():
             pl.semaphore_signal(barrier, inc=1, device_id={"docs": target}, device_id_type=MESH)
 
-    def rows_of(slot, cc, half):
-        first = (slot * CORES + cc) * rows
-        if half is None:
-            return buf.at[pl.ds(pl.multiple_of(first, rows), rows)]
-        return buf.at[pl.ds(pl.multiple_of(first + half * half_rows, half_rows), half_rows)]
-
-    own_data = pltpu.make_async_copy(x_ref, rows_of(0, core, None), own_sem.at[0])
-    own_data.start()
-    own_lab = pltpu.make_async_copy(lab_ref, labs.at[core], own_sem.at[1])
-    own_lab.start()
+    def rows_of(slot, cc, part):
+        first, size = part
+        first = (slot * CORES + cc) * rows + first
+        return buf.at[pl.ds(pl.multiple_of(first, tip), size)]
+
     lower_count = sum(lower.astype(jnp.int32) for lower in down)
     @pl.when(lower_count > 0)
     def _():
         pl.semaphore_wait(barrier, lower_count)
-    for direction, lower in enumerate(down):
-        @pl.when(lower)
-        def _():
-            pl.semaphore_signal(
-                ready_sem.at[AXIS[direction]], inc=1,
-                device_id={"docs": targets[direction]}, device_id_type=MESH,
-            )
-
-    def data_copy(direction, slot, there, half, own=False):
-        if not own:
-            source = rows_of(slot, core, half)
-        else:
-            source = x_ref if half is None else x_ref.at[pl.ds(half * half_rows, half_rows)]
-        done = pair_sem.at[there] if direction == PAIR else recv_sem.at[there * 2 + half]
+
+    def data_copy(direction, slot, there, done, part, own=False):
         return pltpu.make_async_remote_copy(
-            source, rows_of(there, core, half), send_sem.at[direction], done,
+            x_ref.at[pl.ds(*part)] if own else rows_of(slot, core, part), rows_of(there, core, part),
+            send_sem.at[1 if direction == PAIR else 0], done,
             device_id={"docs": targets[direction]}, device_id_type=MESH,
         )
 
-    def lab_copy(direction, slot, there, own=False):
-        there = there * CORES + core
+    def lab_copy(direction, slot, there, done, own=False):
         return pltpu.make_async_remote_copy(
-            lab_ref if own else labs.at[slot * CORES + core], labs.at[there],
-            lsend_sem.at[0], lrecv_sem.at[there],
+            lab_ref if own else labs.at[slot * CORES + core], labs.at[there * CORES + core],
+            lsend_sem.at[0], done,
             device_id={"docs": targets[direction]}, device_id_type=MESH,
         )
+
+    def take(done, data_rows, labels=0):
+        amount = meter.at[pl.ds(0, data_rows * row_units + labels)]
+        pltpu.make_async_remote_copy(
+            amount, amount, lsend_sem.at[0], done,
+            device_id={"docs": targets[PAIR]}, device_id_type=MESH,
+        ).wait_recv()
 
     class Role:
         def __init__(self, is_end):
@@ -375,38 +371,49 @@
         def slot(self, k, other):
             return self.order.index((k, other))
 
-        def there(self, direction, k, other):
+        def done(self, k, other, part):
+            if (k, other) == (3, 1):
+                if self.is_end:
+                    return recv_sem.at[11 if part in (FIRST_TIP, SECOND_TIP) else 10]
+                return recv_sem.at[10 if part == SECOND else 11]
+            if self.is_end:
+                first = {(1, 0): 0, (0, 1): 2, (2, 0): 4, (1, 1): 6, (3, 0): 7, (2, 1): 9}[k, other]
+                split = (k, other) not in ((1, 1), (2, 1))
+            else:
+                first = {(2, 0): 0, (0, 0): 2, (3, 0): 4, (0, 1): 6, (1, 1): 8, (2, 1): 9}[k, other]
+                split = (k, other) not in ((1, 1), (2, 1))
+            return recv_sem.at[first + (1 if split and part == SECOND else 0)]
+
+        def receiver(self, direction, k, other):
             if direction == SIDE:
-                return self.slot(k, 1 - other)
+                return self, k, 1 - other
             if direction == PAIR:
-                return self.slot(k, other)
+                return self, k, other
             if direction == OUT:
-                return END_ORDER.index((k, other))
-            return MID_ORDER.index((k if self.is_end else planes - 1 - k, other))
-
-        def send(self, k, other, half, directions, own=False):
+                return at_end, k, other
+            return at_mid, k if self.is_end else planes - 1 - k, other
+
+        def send(self, k, other, part, directions, own=False):
             for direction in directions:
-                slot, there = self.slot(k, other), self.there(direction, k, other)
-                if half != 1:
-                    lab_copy(direction, slot, there, own).start()
-                data_copy(direction, slot, there, half, own).start()
-
-        def arrived(self, k, other, half):
-            slot = self.slot(k, other)
-            if half == 0:
-                lab_copy(SIDE, slot, slot).wait_recv()
-            data_copy(SIDE, slot, slot, half).wait_recv()
-
-        def pass_on(self, k, other, half, directions):
-            self.arrived(k, other, half)
-            self.send(k, other, half, directions)
+                role, kk, oo = self.receiver(direction, k, other)
+                slot, there = self.slot(k, other), role.slot(kk, oo)
+                done = pair_sem.at[(there + 1) // 2] if direction == PAIR else role.done(kk, oo, part)
+                if part in (FIRST, FIRST_BODY, WHOLE):
+                    lab_copy(direction, slot, there, done, own).start()
+                data_copy(direction, slot, there, done, part, own).start()
+
+        def arrived(self, k, other, part):
+            take(self.done(k, other, part), part[1], 0 if part == SECOND else 1)
+
+        def pass_on(self, k, other, part, directions):
+            self.arrived(k, other, part)
+            self.send(k, other, part, directions)
 
         def pair(self, k, other):
-            self.send(k, other, None, (PAIR,))
+            self.send(k, other, WHOLE, (PAIR,))
 
         def gather(self, k, other):
-            self.arrived(k, other, 1)
-            self.arrived(k, other, 0)
+            self.arrived(k, other, WHOLE)
             self.pair(k, other)
 
     at_end, at_mid = Role(True), Role(False)
@@ -414,8 +421,8 @@
     def start_own(direction):
         def by(role):
             k = 0 if role.is_end else 1
-            for half in {SIDE: (1, 0), PAIR: (None,)}.get(direction, (0, 1)):
-                role.send(k, 0, half, (direction,), own=True)
+            for part in {SIDE: (SECOND, FIRST), PAIR: (WHOLE,)}.get(direction, (FIRST, SECOND)):
+                role.send(k, 0, part, (direction,), own=True)
 
         if direction == OUT:
             by(at_mid)
@@ -429,6 +436,17 @@
         @pl.when(lower)
         def _():
             start_own(direction)
+    for direction, lower in enumerate(down):
+        @pl.when(lower)
+        def _():
+            pl.semaphore_signal(
+                ready_sem.at[AXIS[direction]], inc=1,
+                device_id={"docs": targets[direction]}, device_id_type=MESH,
+            )
+    own_data = pltpu.make_async_copy(x_ref, rows_of(0, core, WHOLE), own_sem.at[0])
+    own_data.start()
+    own_lab = pltpu.make_async_copy(lab_ref, labs.at[core], own_sem.at[1])
+    own_lab.start()
     for direction, higher in reversed(tuple(enumerate(up))):
         @pl.when(higher)
         def _():
@@ -441,17 +459,8 @@
     )[:, :1]
     own_data.wait()
 
-    def from_pair(slot):
-        theirs = slot * CORES + 1 - core
-        pltpu.make_async_remote_copy(
-            labs.at[theirs], labs.at[theirs], lsend_sem.at[0], lrecv_sem.at[theirs],
-            device_id={"docs": targets[PAIR]}, device_id_type=MESH,
-        ).wait_recv()
-        place = rows_of(slot, 1 - core, None)
-        pltpu.make_async_remote_copy(
-            place, place, send_sem.at[PAIR], pair_sem.at[slot],
-            device_id={"docs": targets[PAIR]}, device_id_type=MESH,
-        ).wait_recv()
+    def from_pair(group, slots):
+        take(pair_sem.at[group], slots * rows, slots)
 
     def masked_scores(slot, count):
         keys = count * CORES * rows
@@ -486,65 +495,77 @@
         gained = jnp.dot(weights.astype(jnp.bfloat16), values, preferred_element_type=jnp.float32)
         return peak, total, scale, gained
 
-    from_pair(0)
+    from_pair(0, 1)
     first_block()
 
     def step(j, carry):
         @pl.when(end & (j == 1))
         def _():
             r = at_end
-            r.pass_on(1, 0, 0, (SIDE,))
-            r.pass_on(0, 1, 1, (IN,))
-            r.pass_on(1, 0, 1, (SIDE,))
+            r.pass_on(1, 0, FIRST, (SIDE,))
+            r.pass_on(0, 1, SECOND, (IN,))
+            r.pass_on(1, 0, SECOND, (SIDE,))
             r.pair(1, 0)
-            r.pass_on(0, 1, 0, (IN,))
+            r.pass_on(0, 1, FIRST, (IN,))
             r.pair(0, 1)
-            r.pass_on(2, 0, 0, (SIDE,))
+            r.pass_on(2, 0, FIRST, (SIDE,))
 
         @pl.when(end & (j == 2))
         def _():
             r = at_end
-            r.pass_on(2, 0, 1, (SIDE,))
+            r.pass_on(2, 0, SECOND, (SIDE,))
             r.pair(2, 0)
             r.gather(1, 1)
-            r.pass_on(3, 0, 0, (SIDE,))
+            r.arrived(3, 0, FIRST)
+            r.send(3, 0, FIRST_BODY, (SIDE,))
+            r.send(3, 0, FIRST_TIP, (SIDE,))
 
         @pl.when(end & (j == 3))
         def _():
             r = at_end
-            r.arrived(3, 0, 1)
+            r.arrived(3, 0, SECOND)
             r.pair(3, 0)
             r.gather(2, 1)
+            take(recv_sem.at[10], rows - 2 * tip, 1)
+            r.send(3, 1, FIRST_BODY, (PAIR,))
+            r.send(3, 1, SECOND_BODY, (PAIR,))
+            take(recv_sem.at[11], 2 * tip)
+            r.send(3, 1, TIPS, (PAIR,))
 
         @pl.when(mid & (j == 1))
         def _():
             r = at_mid
-            r.pass_on(2, 0, 0, (OUT, SIDE))
-            r.pass_on(0, 0, 0, (IN,))
-            r.pass_on(2, 0, 1, (OUT, SIDE))
+            r.pass_on(2, 0, FIRST, (OUT, SIDE))
+            r.pass_on(0, 0, FIRST, (IN,))
+            r.pass_on(2, 0, SECOND, (OUT, SIDE))
             r.pair(2, 0)
-            r.pass_on(0, 0, 1, (IN,))
+            r.pass_on(0, 0, SECOND, (IN,))
             r.pair(0, 0)
             r.gather(1, 1)
-            r.pass_on(3, 0, 0, (OUT, SIDE))
-            r.pass_on(0, 1, 1, (IN,))
+            r.pass_on(3, 0, FIRST, (OUT, SIDE))
+            r.pass_on(0, 1, SECOND, (IN,))
 
         @pl.when(mid & (j == 2))
         def _():
             r = at_mid
-            r.pass_on(3, 0, 1, (OUT,))
+            r.pass_on(3, 0, SECOND, (OUT,))
             r.pair(3, 0)
-            r.arrived(0, 1, 0)
+            r.arrived(0, 1, FIRST)
             r.pair(0, 1)
             r.gather(2, 1)
 
         @pl.when(mid & (j == 3))
         def _():
-            at_mid.pass_on(3, 1, 1, (OUT,))
+            r = at_mid
+            r.arrived(3, 1, SECOND)
+            r.send(3, 1, SECOND_BODY, (OUT,))
+            r.send(3, 1, SECOND_TIP, (OUT,))
+            r.send(3, 1, SECOND, (PAIR,))
+            r.arrived(3, 1, FIRST)
+            r.send(3, 1, FIRST, (PAIR,))
 
         slot = 2 * j - 1
-        from_pair(slot)
-        from_pair(slot + 1)
+        from_pair(j, 2)
         peak, total, scale, gained = absorb(slot, 2)
         row_max[...] = peak
         row_total[...] = total
@@ -553,49 +574,30 @@
 
     lax.fori_loop(1, planes, step, 0)
 
-    @pl.when(end)
-    def _():
-        at_end.arrived(3, 1, 1)
-
-    last = at_end
-    last.send(3, 1, 1, (PAIR,))
-    last.arrived(3, 1, 0)
-    last.send(3, 1, 0, (PAIR,))
-    from_pair(last.slot(3, 1))
-    peak, total, scale, gained = absorb(last.slot(3, 1), 1)
+    from_pair(planes, 1)
+    peak, total, scale, gained = absorb(2 * planes - 1, 1)
     density = peak + jnp.log(total)
     dens_ref[...] = jnp.transpose(jnp.broadcast_to(density, (rows, rows)))[:1, :]
     inverse = 1.0 / total
     mean_ref[...] = ((acc[...] * scale + gained) * inverse).astype(mean_ref.dtype)
 
-    def sent(direction, halves):
-        amount = buf.at[pl.ds(0, halves * half_rows)]
+    def sent(done, amount):
         pltpu.make_async_remote_copy(
-            amount, amount, send_sem.at[direction], pair_sem.at[0],
-            device_id={"docs": targets[direction]}, device_id_type=MESH,
-        ).wait_send()
-
-    def labs_sent(count):
-        amount = labs.at[pl.ds(0, count)]
-        pltpu.make_async_remote_copy(
-            amount, amount, lsend_sem.at[0], lrecv_sem.at[0],
+            amount, amount, done, pair_sem.at[0],
             device_id={"docs": targets[PAIR]}, device_id_type=MESH,
         ).wait_send()
 
+    sent(send_sem.at[1], buf.at[pl.ds(0, 16 * half_rows)])
+
     @pl.when(end)
     def _():
-        sent(IN, 4)
-        sent(SIDE, 7)
-        sent(PAIR, 16)
-        labs_sent(14)
+        sent(send_sem.at[0], buf.at[pl.ds(0, 11 * half_rows)])
+        sent(lsend_sem.at[0], labs.at[pl.ds(0, 14)])
 
     @pl.when(mid)
     def _():
-        sent(OUT, 7)
-        sent(IN, 5)
-        sent(SIDE, 5)
-        sent(PAIR, 16)
-        labs_sent(16)
+        sent(send_sem.at[0], buf.at[pl.ds(0, 17 * half_rows)])
+        sent(lsend_sem.at[0], labs.at[pl.ds(0, 16)])
 
 
 def publish_kernel(dens_ref, mean_ref, dens_out, mean_out, sem):
@@ -664,14 +666,14 @@
         scratch_shapes=[
             pltpu.VMEM((device_count * rows, width), jnp.bfloat16),
             pltpu.VMEM((device_count, 1, rows), jnp.int32),
+            pltpu.VMEM((width + CORES, 1, rows), jnp.int32),
             pltpu.VMEM((rows, width), jnp.float32),
             pltpu.VMEM((rows, 1), jnp.float32),
             pltpu.VMEM((rows, 1), jnp.float32),
-            pltpu.SemaphoreType.DMA((4,)),
-            pltpu.SemaphoreType.DMA((2 * chips,)),
-            pltpu.SemaphoreType.DMA((chips,)),
+            pltpu.SemaphoreType.DMA((2,)),
             pltpu.SemaphoreType.DMA((1,)),
-            pltpu.SemaphoreType.DMA((device_count,)),
+            pltpu.SemaphoreType.DMA((12,)),
+            pltpu.SemaphoreType.DMA((chips // 2 + 1,)),
             pltpu.SemaphoreType.DMA((2,)),
             pltpu.SemaphoreType.REGULAR((3,)),
         ],

time: 29 us -> 28 us (0.966)
  Pallas kernels: 28.2 us -> 27.2 us
    pallas_call x1, Pallas kernels: 27.5 us -> 26.5 us  [per_device(): call(device_count, rows, width)(embeddings, labels.reshape(1, rows))]
where the time goes in v5:
time: 28 us; the launch traced here: 27.8 us
  Pallas kernels  27.2 us (97%)
  between operations  0.64 us (2%)
    pallas_call x1, Pallas kernels, per_device(): call(device_count, rows, width)(embeddings, labels.reshape(1, rows))  26.5 us
    pallas_call x1, Pallas kernels, publish(): pl.pallas_call(publish_kernel, out_shape=tuple((jax.ShapeDtypeStruct(a.sh...  0.72 us

profile of v5, /device:TPU:0, one launch (start us, length us, event | category | flops | bytes accessed | tf_op | source)
XLA Modules:
  0.0 27.8 jit_solution(6956990859267543318)
XLA Ops:
  0.6 26.5 %shard_map.41 = (f32[1,128]{1,0:T(1,128)S(1)}, bf16[128,1024]{1,0:T(8,128)(2,1)S(1)}) custom-call(bf16[128,1024]{1,0:T(8,128)(2,1)} %x_ref.1, s32[1,128]{1,0:T(1,128)} %bitcast.2), custom_call_target="tpu_custom_call" | custom-call | tf_op jit(solution)/shard_map/pallas_call | solution.py:687
  27.1 0.7 %shard_map.42 = (f32[1,128]{1,0:T(1,128)}, bf16[128,1024]{1,0:T(8,128)(2,1)}) custom-call(f32[1,128]{1,0:T(1,128)S(1)} %get-tuple-element.6.dens_ref, bf16[128,1024]{1,0:T(8,128)(2,1)S(1)} %get-tuple-element.7.mean_ref), custom_call_target="tpu_custom_call" | custom-call | tf_op jit(solution)/shard_map/pallas_call | solution.py:616

commit v6 on v5

--- a/solution.py
+++ b/solution.py
@@ -297,9 +297,9 @@
     half_rows = rows // 2
     tip = rows // 8
     FIRST, SECOND, WHOLE = (0, half_rows), (half_rows, half_rows), (0, rows)
-    FIRST_BODY, FIRST_TIP = (0, half_rows - tip), (half_rows - tip, tip)
-    SECOND_TIP, SECOND_BODY = (half_rows, tip), (half_rows + tip, half_rows - tip)
-    TIPS = (half_rows - tip, 2 * tip)
+    FIRST_A, FIRST_B = (0, half_rows // 2), (half_rows // 2, half_rows // 2 - tip)
+    FIRST_TIP, SECOND_TIP = (half_rows - tip, tip), (half_rows, tip)
+    SECOND_B, SECOND_A = (half_rows + tip, half_rows // 2 - tip), (rows - half_rows // 2, half_rows // 2)
     me = lax.axis_index("docs")
     core = lax.rem(me, CORES)
     y = lax.rem(me // CORES, 2)
@@ -312,7 +312,7 @@
         zz = jnp.where(mirrored, planes - 1 - k, k)
         return (zz * 2 + column) * CORES + cc
 
-    OUT, IN, SIDE, PAIR = range(4)
+    OUT, IN, SIDE, PAIR, OUT_TWIN, SIDE_TWIN = range(6)
     AXIS = (0, 0, 1, 2)
     home = jnp.where(end, 0, 1)
     targets = (
@@ -320,6 +320,8 @@
         device(home + 1, y, core),
         device(home, 1 - y, core),
         device(home, y, 1 - core),
+        device(0, y, 1 - core),
+        device(home, 1 - y, 1 - core),
     )
     END_ORDER = ((0, 0), (1, 0), (0, 1), (2, 0), (1, 1), (3, 0), (2, 1), (3, 1))
     MID_ORDER = ((1, 0), (2, 0), (0, 0), (3, 0), (0, 1), (1, 1), (2, 1), (3, 1))
@@ -374,7 +376,7 @@
         def done(self, k, other, part):
             if (k, other) == (3, 1):
                 if self.is_end:
-                    return recv_sem.at[11 if part in (FIRST_TIP, SECOND_TIP) else 10]
+                    return recv_sem.at[10 if part in (FIRST_A, SECOND_A) else 11 if part in (FIRST_B, SECOND_B) else 12]
                 return recv_sem.at[10 if part == SECOND else 11]
             if self.is_end:
                 first = {(1, 0): 0, (0, 1): 2, (2, 0): 4, (1, 1): 6, (3, 0): 7, (2, 1): 9}[k, other]
@@ -385,11 +387,11 @@
             return recv_sem.at[first + (1 if split and part == SECOND else 0)]
 
         def receiver(self, direction, k, other):
-            if direction == SIDE:
+            if direction in (SIDE, SIDE_TWIN):
                 return self, k, 1 - other
             if direction == PAIR:
                 return self, k, other
-            if direction == OUT:
+            if direction in (OUT, OUT_TWIN):
                 return at_end, k, other
             return at_mid, k if self.is_end else planes - 1 - k, other
 
@@ -398,7 +400,7 @@
                 role, kk, oo = self.receiver(direction, k, other)
                 slot, there = self.slot(k, other), role.slot(kk, oo)
                 done = pair_sem.at[(there + 1) // 2] if direction == PAIR else role.done(kk, oo, part)
-                if part in (FIRST, FIRST_BODY, WHOLE):
+                if part in (FIRST, FIRST_A, WHOLE):
                     lab_copy(direction, slot, there, done, own).start()
                 data_copy(direction, slot, there, done, part, own).start()
 
@@ -445,7 +447,7 @@
             )
     own_data = pltpu.make_async_copy(x_ref, rows_of(0, core, WHOLE), own_sem.at[0])
     own_data.start()
-    own_lab = pltpu.make_async_copy(lab_ref, labs.at[core], own_sem.at[1])
+    own_lab = pltpu.make_async_copy(lab_ref, labs.at[core], own_sem.at[0])
     own_lab.start()
     for direction, higher in reversed(tuple(enumerate(up))):
         @pl.when(higher)
@@ -453,11 +455,11 @@
             pl.semaphore_wait(ready_sem.at[AXIS[direction]], 1)
             start_own(direction)
 
-    own_lab.wait()
+    own_amount = meter.at[pl.ds(0, rows * row_units + 1)]
+    pltpu.make_async_copy(own_amount, own_amount, own_sem.at[0]).wait()
     label_column = jnp.transpose(
         jnp.broadcast_to(labs[core].astype(jnp.float32), (rows, rows))
     )[:, :1]
-    own_data.wait()
 
     def from_pair(group, slots):
         take(pair_sem.at[group], slots * rows, slots)
@@ -517,8 +519,9 @@
             r.pair(2, 0)
             r.gather(1, 1)
             r.arrived(3, 0, FIRST)
-            r.send(3, 0, FIRST_BODY, (SIDE,))
-            r.send(3, 0, FIRST_TIP, (SIDE,))
+            r.send(3, 0, FIRST_A, (SIDE,))
+            r.send(3, 0, FIRST_B, (SIDE,))
+            r.send(3, 0, FIRST_TIP, (SIDE, SIDE_TWIN))
 
         @pl.when(end & (j == 3))
         def _():
@@ -526,11 +529,12 @@
             r.arrived(3, 0, SECOND)
             r.pair(3, 0)
             r.gather(2, 1)
-            take(recv_sem.at[10], rows - 2 * tip, 1)
-            r.send(3, 1, FIRST_BODY, (PAIR,))
-            r.send(3, 1, SECOND_BODY, (PAIR,))
-            take(recv_sem.at[11], 2 * tip)
-            r.send(3, 1, TIPS, (PAIR,))
+            take(recv_sem.at[10], half_rows, 1)
+            r.send(3, 1, FIRST_A, (PAIR,))
+            r.send(3, 1, SECOND_A, (PAIR,))
+            take(recv_sem.at[11], half_rows - 2 * tip)
+            r.send(3, 1, FIRST_B, (PAIR,))
+            r.send(3, 1, SECOND_B, (PAIR,))
 
         @pl.when(mid & (j == 1))
         def _():
@@ -558,8 +562,9 @@
         def _():
             r = at_mid
             r.arrived(3, 1, SECOND)
-            r.send(3, 1, SECOND_BODY, (OUT,))
-            r.send(3, 1, SECOND_TIP, (OUT,))
+            r.send(3, 1, SECOND_A, (OUT,))
+            r.send(3, 1, SECOND_B, (OUT,))
+            r.send(3, 1, SECOND_TIP, (OUT, OUT_TWIN))
             r.send(3, 1, SECOND, (PAIR,))
             r.arrived(3, 1, FIRST)
             r.send(3, 1, FIRST, (PAIR,))
@@ -574,12 +579,37 @@
 
     lax.fori_loop(1, planes, step, 0)
 
-    from_pair(planes, 1)
-    peak, total, scale, gained = absorb(2 * planes - 1, 1)
+    @pl.when(end)
+    def _():
+        take(recv_sem.at[12], 4 * tip)
+        take(pair_sem.at[planes], rows - 2 * tip, 1)
+
+    @pl.when(mid)
+    def _():
+        from_pair(planes, 1)
+
+    parts = []
+    for cc in range(CORES):
+        values = buf[pl.ds(((2 * planes - 1) * CORES + cc) * rows, rows), :]
+        scores = lax.dot_general(
+            buf[pl.ds(pl.multiple_of(core * rows, rows), rows), :], values,
+            (((1,), (1,)), ((), ())), preferred_element_type=jnp.float32,
+        ) * (kernel_gain / math.sqrt(width))
+        tags = labs[(2 * planes - 1) * CORES + cc].astype(jnp.float32)
+        parts.append((jnp.where(label_column == tags, scores, neg_large), values))
+    before = row_max[...]
+    peak = jnp.maximum(before, jnp.max(jnp.maximum(parts[0][0], parts[1][0]), axis=1, keepdims=True))
+    scale = jnp.exp(before - peak)
+    weights = [jnp.exp(masked - peak) for masked, _ in parts]
+    total = row_total[...] * scale + jnp.sum(weights[0] + weights[1], axis=1, keepdims=True)
+    inverse = 1.0 / total
+    gained = sum(
+        jnp.dot(w.astype(jnp.bfloat16), values, preferred_element_type=jnp.float32)
+        for w, (_, values) in zip(weights, parts)
+    )
+    mean_ref[...] = ((acc[...] * scale + gained) * inverse).astype(mean_ref.dtype)
     density = peak + jnp.log(total)
     dens_ref[...] = jnp.transpose(jnp.broadcast_to(density, (rows, rows)))[:1, :]
-    inverse = 1.0 / total
-    mean_ref[...] = ((acc[...] * scale + gained) * inverse).astype(mean_ref.dtype)
 
     def sent(done, amount):
         pltpu.make_async_remote_copy(
@@ -587,16 +617,16 @@
             device_id={"docs": targets[PAIR]}, device_id_type=MESH,
         ).wait_send()
 
-    sent(send_sem.at[1], buf.at[pl.ds(0, 16 * half_rows)])
-
     @pl.when(end)
     def _():
-        sent(send_sem.at[0], buf.at[pl.ds(0, 11 * half_rows)])
+        sent(send_sem.at[0], buf.at[pl.ds(0, 11 * half_rows + tip)])
+        sent(send_sem.at[1], buf.at[pl.ds(0, 16 * half_rows - 2 * tip)])
         sent(lsend_sem.at[0], labs.at[pl.ds(0, 14)])
 
     @pl.when(mid)
     def _():
-        sent(send_sem.at[0], buf.at[pl.ds(0, 17 * half_rows)])
+        sent(send_sem.at[0], buf.at[pl.ds(0, 17 * half_rows + tip)])
+        sent(send_sem.at[1], buf.at[pl.ds(0, 16 * half_rows)])
         sent(lsend_sem.at[0], labs.at[pl.ds(0, 16)])
 
 
@@ -672,9 +702,9 @@
             pltpu.VMEM((rows, 1), jnp.float32),
             pltpu.SemaphoreType.DMA((2,)),
             pltpu.SemaphoreType.DMA((1,)),
-            pltpu.SemaphoreType.DMA((12,)),
+            pltpu.SemaphoreType.DMA((13,)),
             pltpu.SemaphoreType.DMA((chips // 2 + 1,)),
-            pltpu.SemaphoreType.DMA((2,)),
+            pltpu.SemaphoreType.DMA((1,)),
             pltpu.SemaphoreType.REGULAR((3,)),
         ],
         compiler_params=pltpu.CompilerParams(collective_id=0, has_side_effects=True),

time: 28 us -> 27.8 us (level)
  no operation moved by 1% of the time
where the time goes in v6:
time: 27.8 us; the launch traced here: 27.7 us
  Pallas kernels  27.1 us (97%)
  between operations  0.64 us (2%)
    pallas_call x1, Pallas kernels, per_device(): call(device_count, rows, width)(embeddings, labels.reshape(1, rows))  26.3 us
    pallas_call x1, Pallas kernels, publish(): pl.pallas_call(publish_kernel, out_shape=tuple((jax.ShapeDtypeStruct(a.sh...  0.72 us

profile of v6, /device:TPU:0, one launch (start us, length us, event | category | flops | bytes accessed | tf_op | source)
XLA Modules:
  0.0 27.7 jit_solution(4617296365908902187)
XLA Ops:
  0.6 26.3 %shard_map.41 = (f32[1,128]{1,0:T(1,128)S(1)}, bf16[128,1024]{1,0:T(8,128)(2,1)S(1)}) custom-call(bf16[128,1024]{1,0:T(8,128)(2,1)} %x_ref.1, s32[1,128]{1,0:T(1,128)} %bitcast.2), custom_call_target="tpu_custom_call" | custom-call | tf_op jit(solution)/shard_map/pallas_call | solution.py:717
  27.0 0.7 %shard_map.42 = (f32[1,128]{1,0:T(1,128)}, bf16[128,1024]{1,0:T(8,128)(2,1)}) custom-call(f32[1,128]{1,0:T(1,128)S(1)} %get-tuple-element.6.dens_ref, bf16[128,1024]{1,0:T(8,128)(2,1)S(1)} %get-tuple-element.7.mean_ref), custom_call_target="tpu_custom_call" | custom-call | tf_op jit(solution)/shard_map/pallas_call | solution.py:646

commit v7 on v6

--- a/solution.py
+++ b/solution.py
@@ -300,6 +300,7 @@
     FIRST_A, FIRST_B = (0, half_rows // 2), (half_rows // 2, half_rows // 2 - tip)
     FIRST_TIP, SECOND_TIP = (half_rows - tip, tip), (half_rows, tip)
     SECOND_B, SECOND_A = (half_rows + tip, half_rows // 2 - tip), (rows - half_rows // 2, half_rows // 2)
+    SECOND_C = (half_rows, half_rows // 2)
     me = lax.axis_index("docs")
     core = lax.rem(me, CORES)
     y = lax.rem(me // CORES, 2)
@@ -376,15 +377,17 @@
         def done(self, k, other, part):
             if (k, other) == (3, 1):
                 if self.is_end:
-                    return recv_sem.at[10 if part in (FIRST_A, SECOND_A) else 11 if part in (FIRST_B, SECOND_B) else 12]
-                return recv_sem.at[10 if part == SECOND else 11]
+                    return recv_sem.at[11 if part in (FIRST_A, SECOND_A) else 12 if part in (FIRST_B, SECOND_B) else 13]
+                return recv_sem.at[11 if part == SECOND_A else 12 if part == SECOND_C else 13]
             if self.is_end:
-                first = {(1, 0): 0, (0, 1): 2, (2, 0): 4, (1, 1): 6, (3, 0): 7, (2, 1): 9}[k, other]
-                split = (k, other) not in ((1, 1), (2, 1))
+                first = {(1, 0): 0, (0, 1): 2, (2, 0): 5, (1, 1): 7, (3, 0): 8, (2, 1): 10}[k, other]
             else:
-                first = {(2, 0): 0, (0, 0): 2, (3, 0): 4, (0, 1): 6, (1, 1): 8, (2, 1): 9}[k, other]
-                split = (k, other) not in ((1, 1), (2, 1))
-            return recv_sem.at[first + (1 if split and part == SECOND else 0)]
+                first = {(2, 0): 0, (0, 0): 2, (3, 0): 4, (0, 1): 6, (1, 1): 9, (2, 1): 10}[k, other]
+            if (k, other) in ((1, 1), (2, 1)):
+                return recv_sem.at[first]
+            if (k, other) == (0, 1):
+                return recv_sem.at[first + (0 if part == FIRST else 1 if part == SECOND_A else 2)]
+            return recv_sem.at[first + (1 if part == SECOND else 0)]
 
         def receiver(self, direction, k, other):
             if direction in (SIDE, SIDE_TWIN):
@@ -405,7 +408,7 @@
                 data_copy(direction, slot, there, done, part, own).start()
 
         def arrived(self, k, other, part):
-            take(self.done(k, other, part), part[1], 0 if part == SECOND else 1)
+            take(self.done(k, other, part), part[1], 1 if part[0] == 0 else 0)
 
         def pass_on(self, k, other, part, directions):
             self.arrived(k, other, part)
@@ -423,7 +426,7 @@
     def start_own(direction):
         def by(role):
             k = 0 if role.is_end else 1
-            for part in {SIDE: (SECOND, FIRST), PAIR: (WHOLE,)}.get(direction, (FIRST, SECOND)):
+            for part in {SIDE: (SECOND_A, SECOND_C, FIRST), PAIR: (WHOLE,)}.get(direction, (FIRST, SECOND)):
                 role.send(k, 0, part, (direction,), own=True)
 
         if direction == OUT:
@@ -505,7 +508,8 @@
         def _():
             r = at_end
             r.pass_on(1, 0, FIRST, (SIDE,))
-            r.pass_on(0, 1, SECOND, (IN,))
+            r.pass_on(0, 1, SECOND_A, (IN,))
+            r.pass_on(0, 1, SECOND_C, (IN,))
             r.pass_on(1, 0, SECOND, (SIDE,))
             r.pair(1, 0)
             r.pass_on(0, 1, FIRST, (IN,))
@@ -529,10 +533,10 @@
             r.arrived(3, 0, SECOND)
             r.pair(3, 0)
             r.gather(2, 1)
-            take(recv_sem.at[10], half_rows, 1)
+            take(recv_sem.at[11], half_rows, 1)
             r.send(3, 1, FIRST_A, (PAIR,))
             r.send(3, 1, SECOND_A, (PAIR,))
-            take(recv_sem.at[11], half_rows - 2 * tip)
+            take(recv_sem.at[12], half_rows - 2 * tip)
             r.send(3, 1, FIRST_B, (PAIR,))
             r.send(3, 1, SECOND_B, (PAIR,))
 
@@ -547,7 +551,8 @@
             r.pair(0, 0)
             r.gather(1, 1)
             r.pass_on(3, 0, FIRST, (OUT, SIDE))
-            r.pass_on(0, 1, SECOND, (IN,))
+            r.pass_on(0, 1, SECOND_A, (IN,))
+            r.pass_on(0, 1, SECOND_C, (IN,))
 
         @pl.when(mid & (j == 2))
         def _():
@@ -561,8 +566,9 @@
         @pl.when(mid & (j == 3))
         def _():
             r = at_mid
-            r.arrived(3, 1, SECOND)
+            r.arrived(3, 1, SECOND_A)
             r.send(3, 1, SECOND_A, (OUT,))
+            r.arrived(3, 1, SECOND_C)
             r.send(3, 1, SECOND_B, (OUT,))
             r.send(3, 1, SECOND_TIP, (OUT, OUT_TWIN))
             r.send(3, 1, SECOND, (PAIR,))
@@ -581,7 +587,7 @@
 
     @pl.when(end)
     def _():
-        take(recv_sem.at[12], 4 * tip)
+        take(recv_sem.at[13], 4 * tip)
         take(pair_sem.at[planes], rows - 2 * tip, 1)
 
     @pl.when(mid)
@@ -702,7 +708,7 @@
             pltpu.VMEM((rows, 1), jnp.float32),
             pltpu.SemaphoreType.DMA((2,)),
             pltpu.SemaphoreType.DMA((1,)),
-            pltpu.SemaphoreType.DMA((13,)),
+            pltpu.SemaphoreType.DMA((14,)),
             pltpu.SemaphoreType.DMA((chips // 2 + 1,)),
             pltpu.SemaphoreType.DMA((1,)),
             pltpu.SemaphoreType.REGULAR((3,)),

time: 27.8 us -> 27.7 us (level)
  no operation moved by 1% of the time
where the time goes in v7:
time: 27.7 us; the launch traced here: 27.6 us
  Pallas kernels  26.9 us (97%)
  between operations  0.64 us (2%)
    pallas_call x1, Pallas kernels, per_device(): call(device_count, rows, width)(embeddings, labels.reshape(1, rows))  26.2 us
    pallas_call x1, Pallas kernels, publish(): pl.pallas_call(publish_kernel, out_shape=tuple((jax.ShapeDtypeStruct(a.sh...  0.72 us

profile of v7, /device:TPU:0, one launch (start us, length us, event | category | flops | bytes accessed | tf_op | source)
XLA Modules:
  0.0 27.6 jit_solution(5004600891196859366)
XLA Ops:
  0.6 26.2 %shard_map.41 = (f32[1,128]{1,0:T(1,128)S(1)}, bf16[128,1024]{1,0:T(8,128)(2,1)S(1)}) custom-call(bf16[128,1024]{1,0:T(8,128)(2,1)} %x_ref.1, s32[1,128]{1,0:T(1,128)} %bitcast.2), custom_call_target="tpu_custom_call" | custom-call | tf_op jit(solution)/shard_map/pallas_call | solution.py:723
  26.8 0.7 %shard_map.42 = (f32[1,128]{1,0:T(1,128)}, bf16[128,1024]{1,0:T(8,128)(2,1)}) custom-call(f32[1,128]{1,0:T(1,128)S(1)} %get-tuple-element.6.dens_ref, bf16[128,1024]{1,0:T(8,128)(2,1)S(1)} %get-tuple-element.7.mean_ref), custom_call_target="tpu_custom_call" | custom-call | tf_op jit(solution)/shard_map/pallas_call | solution.py:652

commit v8 on v7

--- a/solution.py
+++ b/solution.py
@@ -290,7 +290,7 @@
 def folded_kernel(
     planes, x_ref, lab_ref, dens_ref, mean_ref,
     buf, labs, meter, acc, row_max, row_total,
-    send_sem, lsend_sem, recv_sem, pair_sem, own_sem, ready_sem,
+    send_sem, recv_sem, pair_sem, own_sem, ready_sem,
 ):
     rows, width = x_ref.shape
     row_units = width * x_ref.dtype.itemsize // (rows * lab_ref.dtype.itemsize)
@@ -314,16 +314,11 @@
         return (zz * 2 + column) * CORES + cc
 
     OUT, IN, SIDE, PAIR, OUT_TWIN, SIDE_TWIN = range(6)
-    AXIS = (0, 0, 1, 2)
+    AXIS = (0, 0, 0, 1)
     home = jnp.where(end, 0, 1)
-    targets = (
-        device(0, y, core),
-        device(home + 1, y, core),
-        device(home, 1 - y, core),
-        device(home, y, 1 - core),
-        device(0, y, 1 - core),
-        device(home, 1 - y, 1 - core),
-    )
+    inward = jnp.where(mirrored, -2 * CORES, 2 * CORES)
+    across, beside = CORES - 2 * CORES * y, 1 - 2 * core
+    targets = (me - inward, me + inward, me + across, me + beside, me - inward + beside, me + across + beside)
     END_ORDER = ((0, 0), (1, 0), (0, 1), (2, 0), (1, 1), (3, 0), (2, 1), (3, 1))
     MID_ORDER = ((1, 0), (2, 0), (0, 0), (3, 0), (0, 1), (1, 1), (2, 1), (3, 1))
 
@@ -348,21 +343,21 @@
     def data_copy(direction, slot, there, done, part, own=False):
         return pltpu.make_async_remote_copy(
             x_ref.at[pl.ds(*part)] if own else rows_of(slot, core, part), rows_of(there, core, part),
-            send_sem.at[1 if direction == PAIR else 0], done,
+            send_sem.at[0], done,
             device_id={"docs": targets[direction]}, device_id_type=MESH,
         )
 
     def lab_copy(direction, slot, there, done, own=False):
         return pltpu.make_async_remote_copy(
             lab_ref if own else labs.at[slot * CORES + core], labs.at[there * CORES + core],
-            lsend_sem.at[0], done,
+            send_sem.at[0], done,
             device_id={"docs": targets[direction]}, device_id_type=MESH,
         )
 
     def take(done, data_rows, labels=0):
         amount = meter.at[pl.ds(0, data_rows * row_units + labels)]
         pltpu.make_async_remote_copy(
-            amount, amount, lsend_sem.at[0], done,
+            amount, amount, send_sem.at[0], done,
             device_id={"docs": targets[PAIR]}, device_id_type=MESH,
         ).wait_recv()
 
@@ -375,19 +370,21 @@
             return self.order.index((k, other))
 
         def done(self, k, other, part):
-            if (k, other) == (3, 1):
-                if self.is_end:
-                    return recv_sem.at[11 if part in (FIRST_A, SECOND_A) else 12 if part in (FIRST_B, SECOND_B) else 13]
-                return recv_sem.at[11 if part == SECOND_A else 12 if part == SECOND_C else 13]
+            second = 1 if part == SECOND else 0
             if self.is_end:
-                first = {(1, 0): 0, (0, 1): 2, (2, 0): 5, (1, 1): 7, (3, 0): 8, (2, 1): 10}[k, other]
+                if (k, other) == (3, 1):
+                    index = 8 if part in (FIRST_A, SECOND_A) else 9 if part in (FIRST_B, SECOND_B) else 10
+                elif (k, other) == (0, 1):
+                    index = {FIRST: 1, SECOND_A: 2, SECOND_C: 3}[part]
+                else:
+                    index = {(1, 0): second, (2, 0): 4 + second, (1, 1): 5, (3, 0): 6 + second, (2, 1): 7}[k, other]
+            elif (k, other) == (3, 1):
+                index = 9 if part == SECOND_A else 10 if part == SECOND_C else 11
+            elif (k, other) == (0, 1):
+                index = {FIRST: 8, SECOND_A: 6, SECOND_C: 7}[part]
             else:
-                first = {(2, 0): 0, (0, 0): 2, (3, 0): 4, (0, 1): 6, (1, 1): 9, (2, 1): 10}[k, other]
-            if (k, other) in ((1, 1), (2, 1)):
-                return recv_sem.at[first]
-            if (k, other) == (0, 1):
-                return recv_sem.at[first + (0 if part == FIRST else 1 if part == SECOND_A else 2)]
-            return recv_sem.at[first + (1 if part == SECOND else 0)]
+                index = {(2, 0): second, (0, 0): 2 + second, (1, 1): 3, (3, 0): 4 + second, (2, 1): 8}[k, other]
+            return recv_sem.at[index]
 
         def receiver(self, direction, k, other):
             if direction in (SIDE, SIDE_TWIN):
@@ -417,10 +414,6 @@
         def pair(self, k, other):
             self.send(k, other, WHOLE, (PAIR,))
 
-        def gather(self, k, other):
-            self.arrived(k, other, WHOLE)
-            self.pair(k, other)
-
     at_end, at_mid = Role(True), Role(False)
 
     def start_own(direction):
@@ -452,10 +445,18 @@
     own_data.start()
     own_lab = pltpu.make_async_copy(lab_ref, labs.at[core], own_sem.at[0])
     own_lab.start()
-    for direction, higher in reversed(tuple(enumerate(up))):
-        @pl.when(higher)
-        def _():
-            pl.semaphore_wait(ready_sem.at[AXIS[direction]], 1)
+    @pl.when(up[PAIR])
+    def _():
+        pl.semaphore_wait(ready_sem.at[1], 1)
+        start_own(PAIR)
+
+    higher_count = sum(higher.astype(jnp.int32) for higher in up[:PAIR])
+    @pl.when(higher_count > 0)
+    def _():
+        pl.semaphore_wait(ready_sem.at[0], higher_count)
+    for direction in (SIDE, IN, OUT):
+        @pl.when(up[direction])
+        def _():
             start_own(direction)
 
     own_amount = meter.at[pl.ds(0, rows * row_units + 1)]
@@ -510,18 +511,20 @@
             r.pass_on(1, 0, FIRST, (SIDE,))
             r.pass_on(0, 1, SECOND_A, (IN,))
             r.pass_on(0, 1, SECOND_C, (IN,))
-            r.pass_on(1, 0, SECOND, (SIDE,))
+            take(r.done(1, 0, SECOND), rows, 1)
+            r.send(1, 0, SECOND, (SIDE,))
+            r.send(0, 1, FIRST, (IN,))
             r.pair(1, 0)
-            r.pass_on(0, 1, FIRST, (IN,))
             r.pair(0, 1)
             r.pass_on(2, 0, FIRST, (SIDE,))
 
         @pl.when(end & (j == 2))
         def _():
             r = at_end
-            r.pass_on(2, 0, SECOND, (SIDE,))
+            take(r.done(2, 0, SECOND), rows + half_rows, 1)
+            r.send(2, 0, SECOND, (SIDE,))
             r.pair(2, 0)
-            r.gather(1, 1)
+            r.pair(1, 1)
             r.arrived(3, 0, FIRST)
             r.send(3, 0, FIRST_A, (SIDE,))
             r.send(3, 0, FIRST_B, (SIDE,))
@@ -530,13 +533,13 @@
         @pl.when(end & (j == 3))
         def _():
             r = at_end
-            r.arrived(3, 0, SECOND)
+            take(r.done(3, 0, SECOND), rows + half_rows, 1)
             r.pair(3, 0)
-            r.gather(2, 1)
-            take(recv_sem.at[11], half_rows, 1)
+            r.pair(2, 1)
+            take(r.done(3, 1, FIRST_A), half_rows, 1)
             r.send(3, 1, FIRST_A, (PAIR,))
             r.send(3, 1, SECOND_A, (PAIR,))
-            take(recv_sem.at[12], half_rows - 2 * tip)
+            take(r.done(3, 1, FIRST_B), half_rows - 2 * tip)
             r.send(3, 1, FIRST_B, (PAIR,))
             r.send(3, 1, SECOND_B, (PAIR,))
 
@@ -547,9 +550,10 @@
             r.pass_on(0, 0, FIRST, (IN,))
             r.pass_on(2, 0, SECOND, (OUT, SIDE))
             r.pair(2, 0)
-            r.pass_on(0, 0, SECOND, (IN,))
+            take(r.done(0, 0, SECOND), rows + half_rows, 1)
+            r.send(0, 0, SECOND, (IN,))
             r.pair(0, 0)
-            r.gather(1, 1)
+            r.pair(1, 1)
             r.pass_on(3, 0, FIRST, (OUT, SIDE))
             r.pass_on(0, 1, SECOND_A, (IN,))
             r.pass_on(0, 1, SECOND_C, (IN,))
@@ -559,9 +563,9 @@
             r = at_mid
             r.pass_on(3, 0, SECOND, (OUT,))
             r.pair(3, 0)
-            r.arrived(0, 1, FIRST)
+            take(r.done(0, 1, FIRST), rows + half_rows, 2)
             r.pair(0, 1)
-            r.gather(2, 1)
+            r.pair(2, 1)
 
         @pl.when(mid & (j == 3))
         def _():
@@ -587,7 +591,7 @@
 
     @pl.when(end)
     def _():
-        take(recv_sem.at[13], 4 * tip)
+        take(at_end.done(3, 1, FIRST_TIP), 4 * tip)
         take(pair_sem.at[planes], rows - 2 * tip, 1)
 
     @pl.when(mid)
@@ -617,23 +621,20 @@
     density = peak + jnp.log(total)
     dens_ref[...] = jnp.transpose(jnp.broadcast_to(density, (rows, rows)))[:1, :]
 
-    def sent(done, amount):
+    def sent(data_rows, labels):
+        amount = meter.at[pl.ds(0, data_rows * row_units + labels)]
         pltpu.make_async_remote_copy(
-            amount, amount, done, pair_sem.at[0],
+            amount, amount, send_sem.at[0], pair_sem.at[0],
             device_id={"docs": targets[PAIR]}, device_id_type=MESH,
         ).wait_send()
 
     @pl.when(end)
     def _():
-        sent(send_sem.at[0], buf.at[pl.ds(0, 11 * half_rows + tip)])
-        sent(send_sem.at[1], buf.at[pl.ds(0, 16 * half_rows - 2 * tip)])
-        sent(lsend_sem.at[0], labs.at[pl.ds(0, 14)])
+        sent(27 * half_rows - tip, 14)
 
     @pl.when(mid)
     def _():
-        sent(send_sem.at[0], buf.at[pl.ds(0, 17 * half_rows + tip)])
-        sent(send_sem.at[1], buf.at[pl.ds(0, 16 * half_rows)])
-        sent(lsend_sem.at[0], labs.at[pl.ds(0, 16)])
+        sent(33 * half_rows + tip, 16)
 
 
 def publish_kernel(dens_ref, mean_ref, dens_out, mean_out, sem):
@@ -702,16 +703,15 @@
         scratch_shapes=[
             pltpu.VMEM((device_count * rows, width), jnp.bfloat16),
             pltpu.VMEM((device_count, 1, rows), jnp.int32),
-            pltpu.VMEM((width + CORES, 1, rows), jnp.int32),
+            pltpu.VMEM(((33 * rows // 2 + rows // 8) * width // (2 * rows) + 2 * chips, 1, rows), jnp.int32),
             pltpu.VMEM((rows, width), jnp.float32),
             pltpu.VMEM((rows, 1), jnp.float32),
             pltpu.VMEM((rows, 1), jnp.float32),
-            pltpu.SemaphoreType.DMA((2,)),
             pltpu.SemaphoreType.DMA((1,)),
-            pltpu.SemaphoreType.DMA((14,)),
+            pltpu.SemaphoreType.DMA((12,)),
             pltpu.SemaphoreType.DMA((chips // 2 + 1,)),
             pltpu.SemaphoreType.DMA((1,)),
-            pltpu.SemaphoreType.REGULAR((3,)),
+            pltpu.SemaphoreType.REGULAR((2,)),
         ],
         compiler_params=pltpu.CompilerParams(collective_id=0, has_side_effects=True),
     )

time: 27.7 us -> 27.7 us (level)
  no operation moved by 1% of the time
where the time goes in v8:
time: 27.7 us; the launch traced here: 27.5 us
  Pallas kernels  26.9 us (97%)
  between operations  0.64 us (2%)
    pallas_call x1, Pallas kernels, per_device(): call(device_count, rows, width)(embeddings, labels.reshape(1, rows))  26.1 us
    pallas_call x1, Pallas kernels, publish(): pl.pallas_call(publish_kernel, out_shape=tuple((jax.ShapeDtypeStruct(a.sh...  0.72 us

profile of v8, /device:TPU:0, one launch (start us, length us, event | category | flops | bytes accessed | tf_op | source)
XLA Modules:
  0.0 27.5 jit_solution(15433797325656446568)
XLA Ops:
  0.6 26.1 %shard_map.41 = (f32[1,128]{1,0:T(1,128)S(1)}, bf16[128,1024]{1,0:T(8,128)(2,1)S(1)}) custom-call(bf16[128,1024]{1,0:T(8,128)(2,1)} %x_ref.1, s32[1,128]{1,0:T(1,128)} %bitcast.2), custom_call_target="tpu_custom_call" | custom-call | tf_op jit(solution)/shard_map/pallas_call | solution.py:723
  26.8 0.7 %shard_map.42 = (f32[1,128]{1,0:T(1,128)}, bf16[128,1024]{1,0:T(8,128)(2,1)}) custom-call(f32[1,128]{1,0:T(1,128)S(1)} %get-tuple-element.6.dens_ref, bf16[128,1024]{1,0:T(8,128)(2,1)S(1)} %get-tuple-element.7.mean_ref), custom_call_target="tpu_custom_call" | custom-call | tf_op jit(solution)/shard_map/pallas_call | solution.py:653

commit v9 on v8

--- a/solution.py
+++ b/solution.py
@@ -305,6 +305,12 @@
     core = lax.rem(me, CORES)
     y = lax.rem(me // CORES, 2)
     z = me // (CORES * 2)
+    barrier = pltpu.get_barrier_semaphore()
+    for higher, stride in ((z < planes - 1, 2 * CORES), (y == 0, CORES), (core == 0, 1)):
+        @pl.when(higher)
+        def _():
+            pl.semaphore_signal(barrier, inc=1, device_id={"docs": me + stride}, device_id_type=MESH)
+
     mirrored = 2 * z >= planes
     end = (z == 0) | (z == planes - 1)
     mid = jnp.logical_not(end)
@@ -314,7 +320,6 @@
         return (zz * 2 + column) * CORES + cc
 
     OUT, IN, SIDE, PAIR, OUT_TWIN, SIDE_TWIN = range(6)
-    AXIS = (0, 0, 0, 1)
     home = jnp.where(end, 0, 1)
     inward = jnp.where(mirrored, -2 * CORES, 2 * CORES)
     across, beside = CORES - 2 * CORES * y, 1 - 2 * core
@@ -324,18 +329,13 @@
 
     up = (mid & mirrored, jnp.logical_not(mirrored), y == 0, core == 0)
     down = (mid & jnp.logical_not(mirrored), mirrored, y == 1, core == 1)
-    barrier = pltpu.get_barrier_semaphore()
-    for target, higher in zip(targets, up):
-        @pl.when(higher)
-        def _():
-            pl.semaphore_signal(barrier, inc=1, device_id={"docs": target}, device_id_type=MESH)
 
     def rows_of(slot, cc, part):
         first, size = part
         first = (slot * CORES + cc) * rows + first
         return buf.at[pl.ds(pl.multiple_of(first, tip), size)]
 
-    lower_count = sum(lower.astype(jnp.int32) for lower in down)
+    lower_count = (z > 0).astype(jnp.int32) + y + core
     @pl.when(lower_count > 0)
     def _():
         pl.semaphore_wait(barrier, lower_count)
@@ -434,13 +434,13 @@
         @pl.when(lower)
         def _():
             start_own(direction)
-    for direction, lower in enumerate(down):
+    for lower, stride, axis in ((z > 0, 2 * CORES, 0), (y == 1, CORES, 0), (core == 1, 1, 1)):
         @pl.when(lower)
         def _():
             pl.semaphore_signal(
-                ready_sem.at[AXIS[direction]], inc=1,
-                device_id={"docs": targets[direction]}, device_id_type=MESH,
+                ready_sem.at[axis], inc=1, device_id={"docs": me - stride}, device_id_type=MESH,
             )
+
     own_data = pltpu.make_async_copy(x_ref, rows_of(0, core, WHOLE), own_sem.at[0])
     own_data.start()
     own_lab = pltpu.make_async_copy(lab_ref, labs.at[core], own_sem.at[0])
@@ -613,9 +613,9 @@
     weights = [jnp.exp(masked - peak) for masked, _ in parts]
     total = row_total[...] * scale + jnp.sum(weights[0] + weights[1], axis=1, keepdims=True)
     inverse = 1.0 / total
-    gained = sum(
-        jnp.dot(w.astype(jnp.bfloat16), values, preferred_element_type=jnp.float32)
-        for w, (_, values) in zip(weights, parts)
+    gained = jnp.dot(
+        jnp.concatenate([w.astype(jnp.bfloat16) for w in weights], axis=1),
+        buf[pl.ds((2 * planes - 1) * CORES * rows, CORES * rows), :], preferred_element_type=jnp.float32,
     )
     mean_ref[...] = ((acc[...] * scale + gained) * inverse).astype(mean_ref.dtype)
     density = peak + jnp.log(total)

time: 27.7 us -> 27.6 us (level)
  no operation moved by 1% of the time
where the time goes in v9:
time: 27.6 us; the launch traced here: 27.5 us
  Pallas kernels  26.9 us (97%)
  between operations  0.64 us (2%)
    pallas_call x1, Pallas kernels, per_device(): call(device_count, rows, width)(embeddings, labels.reshape(1, rows))  26.1 us
    pallas_call x1, Pallas kernels, publish(): pl.pallas_call(publish_kernel, out_shape=tuple((jax.ShapeDtypeStruct(a.sh...  0.72 us

profile of v9, /device:TPU:0, one launch (start us, length us, event | category | flops | bytes accessed | tf_op | source)
XLA Modules:
  0.0 27.5 jit_solution(6721485075885794148)
XLA Ops:
  0.6 26.1 %shard_map.41 = (f32[1,128]{1,0:T(1,128)S(1)}, bf16[128,1024]{1,0:T(8,128)(2,1)S(1)}) custom-call(bf16[128,1024]{1,0:T(8,128)(2,1)} %x_ref.1, s32[1,128]{1,0:T(1,128)} %bitcast.2), custom_call_target="tpu_custom_call" | custom-call | tf_op jit(solution)/shard_map/pallas_call | solution.py:723
  26.8 0.7 %shard_map.42 = (f32[1,128]{1,0:T(1,128)}, bf16[128,1024]{1,0:T(8,128)(2,1)}) custom-call(f32[1,128]{1,0:T(1,128)S(1)} %get-tuple-element.6.dens_ref, bf16[128,1024]{1,0:T(8,128)(2,1)S(1)} %get-tuple-element.7.mean_ref), custom_call_target="tpu_custom_call" | custom-call | tf_op jit(solution)/shard_map/pallas_call | solution.py:653

commit v10 on v9

--- a/solution.py
+++ b/solution.py
@@ -491,14 +491,21 @@
         acc[...] = jnp.dot(weights.astype(jnp.bfloat16), values, preferred_element_type=jnp.float32)
 
     def absorb(slot, count):
-        scores, near, values = masked_scores(slot, count)
-        masked = jnp.where(near, scores, neg_large)
+        parts = []
+        for n in range(count):
+            scores, near, values = masked_scores(slot + n, 1)
+            parts.append((jnp.where(near, scores, neg_large), values))
         before = row_max[...]
-        peak = jnp.maximum(before, jnp.max(masked, axis=1, keepdims=True))
-        weights = jnp.exp(masked - peak)
+        peak = before
+        for masked, _ in parts:
+            peak = jnp.maximum(peak, jnp.max(masked, axis=1, keepdims=True))
+        weights = [jnp.exp(masked - peak) for masked, _ in parts]
         scale = jnp.exp(before - peak)
-        total = row_total[...] * scale + jnp.sum(weights, axis=1, keepdims=True)
-        gained = jnp.dot(weights.astype(jnp.bfloat16), values, preferred_element_type=jnp.float32)
+        total = row_total[...] * scale + jnp.sum(sum(weights), axis=1, keepdims=True)
+        gained = sum(
+            jnp.dot(w.astype(jnp.bfloat16), values, preferred_element_type=jnp.float32)
+            for w, (_, values) in zip(weights, parts)
+        )
         return peak, total, scale, gained
 
     from_pair(0, 1)

time: 27.6 us -> 27.6 us (level)
  no operation moved by 1% of the time
where the time goes in v10:
time: 27.6 us; the launch traced here: 27.5 us
  Pallas kernels  26.8 us (97%)
  between operations  0.64 us (2%)
    pallas_call x1, Pallas kernels, per_device(): call(device_count, rows, width)(embeddings, labels.reshape(1, rows))  26.1 us
    pallas_call x1, Pallas kernels, publish(): pl.pallas_call(publish_kernel, out_shape=tuple((jax.ShapeDtypeStruct(a.sh...  0.72 us

profile of v10, /device:TPU:0, one launch (start us, length us, event | category | flops | bytes accessed | tf_op | source)
XLA Modules:
  0.0 27.5 jit_solution(4927075335572631321)
XLA Ops:
  0.6 26.1 %shard_map.41 = (f32[1,128]{1,0:T(1,128)S(1)}, bf16[128,1024]{1,0:T(8,128)(2,1)S(1)}) custom-call(bf16[128,1024]{1,0:T(8,128)(2,1)} %x_ref.1, s32[1,128]{1,0:T(1,128)} %bitcast.2), custom_call_target="tpu_custom_call" | custom-call | tf_op jit(solution)/shard_map/pallas_call | solution.py:730
  26.8 0.7 %shard_map.42 = (f32[1,128]{1,0:T(1,128)}, bf16[128,1024]{1,0:T(8,128)(2,1)}) custom-call(f32[1,128]{1,0:T(1,128)S(1)} %get-tuple-element.6.dens_ref, bf16[128,1024]{1,0:T(8,128)(2,1)S(1)} %get-tuple-element.7.mean_ref), custom_call_target="tpu_custom_call" | custom-call | tf_op jit(solution)/shard_map/pallas_call | solution.py:660

commit v11 on v10

--- a/solution.py
+++ b/solution.py
@@ -290,7 +290,7 @@
 def folded_kernel(
     planes, x_ref, lab_ref, dens_ref, mean_ref,
     buf, labs, meter, acc, row_max, row_total,
-    send_sem, recv_sem, pair_sem, own_sem, ready_sem,
+    send_sem, recv_sem, pair_sem, ready_sem,
 ):
     rows, width = x_ref.shape
     row_units = width * x_ref.dtype.itemsize // (rows * lab_ref.dtype.itemsize)
@@ -441,9 +441,9 @@
                 ready_sem.at[axis], inc=1, device_id={"docs": me - stride}, device_id_type=MESH,
             )
 
-    own_data = pltpu.make_async_copy(x_ref, rows_of(0, core, WHOLE), own_sem.at[0])
+    own_data = pltpu.make_async_copy(x_ref, rows_of(0, core, WHOLE), pair_sem.at[0])
     own_data.start()
-    own_lab = pltpu.make_async_copy(lab_ref, labs.at[core], own_sem.at[0])
+    own_lab = pltpu.make_async_copy(lab_ref, labs.at[core], pair_sem.at[0])
     own_lab.start()
     @pl.when(up[PAIR])
     def _():
@@ -459,8 +459,7 @@
         def _():
             start_own(direction)
 
-    own_amount = meter.at[pl.ds(0, rows * row_units + 1)]
-    pltpu.make_async_copy(own_amount, own_amount, own_sem.at[0]).wait()
+    take(pair_sem.at[0], 2 * rows, 2)
     label_column = jnp.transpose(
         jnp.broadcast_to(labs[core].astype(jnp.float32), (rows, rows))
     )[:, :1]
@@ -508,7 +507,6 @@
         )
         return peak, total, scale, gained
 
-    from_pair(0, 1)
     first_block()
 
     def step(j, carry):
@@ -717,7 +715,6 @@
             pltpu.SemaphoreType.DMA((1,)),
             pltpu.SemaphoreType.DMA((12,)),
             pltpu.SemaphoreType.DMA((chips // 2 + 1,)),
-            pltpu.SemaphoreType.DMA((1,)),
             pltpu.SemaphoreType.REGULAR((2,)),
         ],
         compiler_params=pltpu.CompilerParams(collective_id=0, has_side_effects=True),

time: 27.6 us -> 27.6 us (level)
  no operation moved by 1% of the time
where the time goes in v11:
time: 27.6 us; the launch traced here: 27.5 us
  Pallas kernels  26.8 us (97%)
  between operations  0.64 us (2%)
    pallas_call x1, Pallas kernels, per_device(): call(device_count, rows, width)(embeddings, labels.reshape(1, rows))  26.1 us
    pallas_call x1, Pallas kernels, publish(): pl.pallas_call(publish_kernel, out_shape=tuple((jax.ShapeDtypeStruct(a.sh...  0.72 us

profile of v11, /device:TPU:0, one launch (start us, length us, event | category | flops | bytes accessed | tf_op | source)
XLA Modules:
  0.0 27.5 jit_solution(6654853407739340042)
XLA Ops:
  0.6 26.1 %shard_map.41 = (f32[1,128]{1,0:T(1,128)S(1)}, bf16[128,1024]{1,0:T(8,128)(2,1)S(1)}) custom-call(bf16[128,1024]{1,0:T(8,128)(2,1)} %x_ref.1, s32[1,128]{1,0:T(1,128)} %bitcast.2), custom_call_target="tpu_custom_call" | custom-call | tf_op jit(solution)/shard_map/pallas_call | solution.py:727
  26.8 0.7 %shard_map.42 = (f32[1,128]{1,0:T(1,128)}, bf16[128,1024]{1,0:T(8,128)(2,1)}) custom-call(f32[1,128]{1,0:T(1,128)S(1)} %get-tuple-element.6.dens_ref, bf16[128,1024]{1,0:T(8,128)(2,1)S(1)} %get-tuple-element.7.mean_ref), custom_call_target="tpu_custom_call" | custom-call | tf_op jit(solution)/shard_map/pallas_call | solution.py:658
